TPU v7x, 128 devices: a whole 4x4x4 slice. The times are simulated.
128 devices in a mesh: gz: 8 (over x, core), xy: 16 (over y, z).
Axes of the slice: x: 4, y: 4, z: 4, core: 2. Of those that a mesh axis runs over, the one named last changes fastest.
Arguments:
- volume: bfloat16 [256, 64, 40960], P('gz', None, 'xy'), may hold values from -6 to 6
- occupancy: int32 [8, 320], P('gz', 'xy'), may hold values from 0 to 1, as said below
- device_order: int32 [8, 16], P('gz'), may hold values from 0 to 15, each once within a row
- weight_one: bfloat16 [64, 576], replicated, may hold values from -0.25 to 0.25
- bias_one: float32 [64], replicated, may hold values from -3 to 3
- weight_two: bfloat16 [64, 1728], replicated, may hold values from -0.15625 to 0.15625
- bias_two: float32 [64], replicated, may hold values from -3 to 3
Outputs:
- features: bfloat16 [1280, 64, 512], P(('gz', 'xy'))
Inputs may be any that keep to these rules, and one draw needn't show every extreme that they name: `occupancy`: each slab holds exactly 160 tissue bricks, and in each slab all 20 bricks of one xy index are tissue. `device_order`: each slab's row names every xy index once.
All inputs are finite; a program needn't handle non-finite values.
Results may differ from a plain program's by a relative error of at most 0.0025.
Values may be sent and summed in bfloat16 or wider, within the bound.
No kernel may reach another device: no remote copies, remote signals or barrier semaphores. Data moves between devices by JAX's collectives and lax.ppermute only.
A program may use at most 256 MiB of HBM per device.

v0:
```python
import jax
import jax.numpy as jnp
from jax import lax
from jax.sharding import PartitionSpec as P


def padded(value, sides, width):
    for axis, dim in sides:
        peers, length = (lax.axis_size(axis), value.shape[dim])
        up = [(i, (i + 1) % peers) for i in range(peers - 1)]
        down = [(j, i) for i, j in up]
        last = lax.slice_in_dim(value, length - width, length, axis=dim)
        leading = lax.slice_in_dim(value, 0, width, axis=dim)
        before = lax.ppermute(last, axis, up)
        after = lax.ppermute(leading, axis, down)
        value = jnp.concatenate([before, value, after], axis=dim)
    return value


def zone_table(length):
    position = jnp.arange(length)
    lower_end = (position == 0).astype(jnp.float32)
    upper_end = (position == length - 1).astype(jnp.float32)
    middle = 1.0 - lower_end - upper_end
    return jnp.stack([lower_end, middle, upper_end], axis=1)


def conv_chain(extended, flags, weight_one, bias_one, weight_two, bias_two):
    count, layers, channels, rows_ext, across = extended.shape
    inner_size = layers - 2
    kernel_one = weight_one.reshape(channels, 1, 3, 3, channels)
    first_sum = lax.conv_general_dilated(
        extended,
        kernel_one,
        (1, 1, 1),
        ((0, 0), (0, 0), (1, 1)),
        dimension_numbers=("NDCHW", "ODHWI", "NCDHW"),
        preferred_element_type=jnp.float32,
    )
    first_act = jax.nn.relu(first_sum + bias_one[None, :, None, None, None])
    region = jnp.einsum(
        "za,nab,yb->nzy", zone_table(layers), flags.astype(jnp.float32), zone_table(inner_size + 2)
    )
    hidden = (first_act * region[:, None, :, :, None]).astype(jnp.bfloat16)
    kernel_two = weight_two.reshape(channels, 3, 3, 3, channels)
    second_sum = lax.conv_general_dilated(
        hidden,
        kernel_two,
        (1, 1, 1),
        ((0, 0), (0, 0), (1, 1)),
        dimension_numbers=("NCDHW", "ODHWI", "NCDHW"),
        preferred_element_type=jnp.float32,
    )
    second_act = jax.nn.relu(second_sum + bias_two[None, :, None, None, None])
    second_act = second_act.reshape(
        count, channels, inner_size // 2, 2, inner_size // 2, 2, across // 2, 2
    )
    pooled = jnp.mean(second_act, axis=(3, 5, 7))
    return pooled.reshape(count, channels, -1).astype(jnp.bfloat16)


def per_device(volume, occupancy, device_order, weight_one, bias_one, weight_two, bias_two):
    brick_side, channels, span = volume.shape
    columns = occupancy.shape[1]
    across = span // (columns * brick_side)
    groups = lax.axis_size("xy")
    capacity = (columns + groups - 1) // groups
    slot_count = columns // 2
    brick_span = brick_side * across
    tissue_row = occupancy[0]
    indicator = jnp.repeat(tissue_row.astype(jnp.bfloat16), brick_span)
    masked = volume * indicator[None, None, :]
    tissue_halo = padded(occupancy, (("gz", 0), ("xy", 1)), 1)
    z_extended = padded(masked, (("gz", 0),), 1)
    full_rims = padded(z_extended, (("xy", 2),), 2 * across)
    own_count = jnp.sum(tissue_row).reshape(1)
    all_counts = lax.all_gather(own_count, "xy", axis=0, tiled=True)
    own_index = lax.axis_index("xy")
    label_ids = jnp.arange(groups, dtype=jnp.int32)
    starts = jnp.cumsum(all_counts) - all_counts
    own_start = jnp.sum(jnp.where(label_ids == own_index, starts, 0))
    local_rank = jnp.cumsum(tissue_row) - tissue_row
    global_index = own_start + local_rank
    label_of = global_index % groups
    order_row = device_order[0]
    destination = jnp.sum(
        jnp.where(label_of[:, None] == label_ids[None, :], order_row[None, :], 0), axis=1
    )
    slot_out = destination * capacity + local_rank // groups
    buffer_ids = jnp.arange(groups * capacity, dtype=jnp.int32)
    matches = (slot_out[None, :] == buffer_ids[:, None]) & (tissue_row[None, :] > 0)
    source_column = jnp.sum(
        jnp.where(matches, jnp.arange(columns, dtype=jnp.int32)[None, :], 0), axis=1
    )
    own_label = jnp.sum(jnp.where(order_row == own_index, label_ids, 0))
    wanted_index = jnp.arange(slot_count, dtype=jnp.int32) * groups + own_label
    range_ends = starts + all_counts
    anchor_device = jnp.sum(
        (range_ends[None, :] <= wanted_index[:, None]).astype(jnp.int32), axis=1
    )
    anchor_start = jnp.sum(
        jnp.where(label_ids[None, :] == anchor_device[:, None], starts[None, :], 0), axis=1
    )
    arrival = anchor_device * capacity + (wanted_index - anchor_start) // groups

    def cut_brick(column_index):
        return lax.dynamic_slice_in_dim(
            full_rims, column_index * brick_span, (brick_side + 4) * across, 2
        )

    def cut_flags(column_index):
        return lax.dynamic_slice(tissue_halo, (jnp.int32(0), column_index), (3, 3)).astype(
            jnp.bfloat16
        )

    picked = jax.vmap(cut_brick)(source_column)
    picked_flags = jax.vmap(cut_flags)(source_column)
    arrived, arrived_flags = (
        lax.all_to_all(picked, "xy", split_axis=0, concat_axis=0, tiled=True),
        lax.all_to_all(picked_flags, "xy", split_axis=0, concat_axis=0, tiled=True),
    )
    chosen_bricks = jnp.take(arrived, arrival, axis=0)
    chosen_flags = jnp.take(arrived_flags, arrival, axis=0)
    shaped = chosen_bricks.reshape(
        chosen_bricks.shape[0], brick_side + 2, channels, brick_side + 4, across
    )
    return conv_chain(shaped, chosen_flags, weight_one, bias_one, weight_two, bias_two)


def solution(mesh):
    in_specs = (P("gz", None, "xy"), P("gz", "xy"), P("gz", None), P(), P(), P(), P())
    out_specs = P(("gz", "xy"), None, None)
    return jax.shard_map(
        per_device, mesh=mesh, in_specs=in_specs, out_specs=out_specs, check_vma=False
    )
```

profile of v0, /device:TPU:0, one launch (start us, length us, event | category | flops | bytes accessed | tf_op | source)
XLA Modules:
  0.0 1161.9 jit_solution(4842804171284765545)
XLA Ops:
  0.0 1.4 collective-permute-start.4
  1.4 1.4 reduce_sum.76
  4.0 1.4 dynamic-update-slice.2
  6.7 18.0 %all-reduce.2 = s32[16]{0:T(128)S(1)} all-reduce(s32[16]{0:T(128)S(1)} %dynamic-update-slice.2), channel_id=1, replica_groups=mesh['gz'=8,'xy'=16] {'xy'}, use_global_device_ids=true, to_apply=%add.2 | all-reduce | flops 16 | bytes 128
  26.5 1.4 and_select_fusion.2
  29.4 5.5 broadcast_multiply_fusion
  34.9 4.0 copy-done.1
  38.9 1.3 collective-permute-start
  40.2 1.3 collective-permute-start.1
  41.8 2.9 collective-permute-start.6
  44.7 1.3 collective-permute-start.7
  46.0 4.2 collective-permute-done.7
  50.3 5.9 pad_maximum_fusion.1
  56.1 4.1 copy-done
  60.7 1.9 collective-permute-start.2
  62.9 1.3 collective-permute-start.3
  64.2 46.0 %while.1 = (s32[]{:T(128)}, s32[3,22]{1,0:T(4,128)S(1)}, s32[32,2]{0,1:T(2,128)S(1)}, s32[32,3,3]{2,1,0:T(4,128)S(1)}, s32[]{:T(128)}) while((s32[]{:T(128)}, s32[3,22]{1,0:T(4,128)S(1)}, s32[32,2]{0,1:T(2,128)S(1)}, s32[32,3,3]{2,1,0:T(4,128)S(1)}, s32[]{:T(128)}) %tuple.23), condition=%wide.while_cond, body=%wide.while_body.sunk | while | flops 2 | bytes 4193 | solution.py:112
  110.8 8.9 all-to-all-start.1
  119.7 27.6 %copy.86 = bf16[34,64,2560]{1,0,2:T(8,128)(2,1)} copy(bf16[34,64,2560]{2,1,0:T(8,128)(2,1)} %copy-done) | data formatting | bytes 22282240 | tf_op jit(solution)/shard_map/concatenate | solution.py:16
  147.4 30.5 %pad_maximum_fusion = bf16[34,64,2576]{1,0,2:T(8,128)(2,1)} fusion(bf16[34,64,8]{1,0,2:T(8,128)(2,1)S(1)} %copy.87, bf16[34,64,2560]{1,0,2:T(8,128)(2,1)} %copy.86, bf16[34,64,8]{1,0,2:T(8,128)(2,1)S(1)} %copy.85), kind=kLoop, calls=%fused_computation.7 | loop fusion | flops 11210752 | bytes 22421504 | tf_op jit(solution)/shard_map/concatenate | solution.py:16
  177.9 24.9 %gather_fusion = bf16[32,34,64,144]{2,1,3,0:T(8,128)(2,1)} fusion(bf16[34,64,2576]{1,0,2:T(8,128)(2,1)} %pad_maximum_fusion, s32[32]{0:T(128)S(1)} %get-tuple-element.30), kind=kCustom, calls=%fused_computation | custom fusion | bytes 40108416 | tf_op jit(solution)/shard_map/vmap()/gather | solution.py:107
  202.8 66.3 %copy.89 = bf16[32,34,64,144]{3,2,1,0:T(8,128)(2,1)} copy(bf16[32,34,64,144]{2,1,3,0:T(8,128)(2,1)} %gather_fusion) | data formatting | bytes 40108032 | tf_op jit(solution)/shard_map/vmap()/gather | solution.py:107
  269.1 7.5 all-to-all-start
  281.7 661.8 %all-to-all-done = bf16[32,34,64,144]{3,2,1,0:T(8,128)(2,1)} async-done(((bf16[32,34,64,144]{3,2,1,0:T(8,128)(2,1)}), bf16[32,34,64,144]{3,2,1,0:T(8,128)(2,1)}, u32[]{:S(2)}, u32[]{:S(2)}) %all-to-all-start) | async-done | bytes 20054048 | tf_op jit(solution)/shard_map/all_to_all | solution.py:119
  943.6 10.3 gather_fusion.1
  953.9 16.4 %copy.90 = bf16[10,34,64,144]{2,3,1,0:T(8,128)(2,1)} copy(bf16[10,34,64,144]{3,2,1,0:T(8,128)(2,1)} %gather_fusion.1) | data formatting | bytes 12533760 | tf_op jit(solution)/shard_map/jit(_take)/gather | solution.py:122
  970.3 8.6 broadcast_select_fusion
  978.9 29.9 %fusion = f32[10,64,34,34,4]{1,0,4,3,2:T(8,128)} fusion(bf16[64,1,3,3,64]{0,4,3,2,1:T(8,128)(2,1)S(1)} %bitcast.64, bf16[10,34,64,36,4]{2,4,3,1,0:T(4,128)(2,1)S(1)} %broadcast_select_fusion), kind=kOutput, calls=%fused_computation.8 | convolution fusion | flops 2840985600 | bytes 18178048 | tf_op jit(solution)/shard_map/conv_general_dilated | solution.py:32
  1008.8 131.4 %add_maximum_fusion = f32[10,64,32,32,4]{1,0,4,3,2:T(8,128)} fusion(f32[10,64,34,34,4]{1,0,4,3,2:T(8,128)} %fusion, f32[10,34,34]{0,2,1:T(8,128)S(1)} %copy.95, f32[64]{0:T(128)S(1)} %copy-done.6, f32[64]{0:T(128)S(1)} %copy-done.7, bf16[64,3,3,3,64]{4,3,2,1,0:T(4,128)(2,1)S(1)} %reshape.241), kind=kOutput, calls=%fused_computation.6 | convolution fusion | flops 7566827520 | bytes 22591136 | tf_op jit(solution)/shard_map/conv_general_dilated | solution.py:46
  1140.2 15.3 %reduce_sum.85 = f32[10,64,16,16,2]{1,0,4,3,2:T(8,128)} reduce(f32[10,64,16,2,16,2,2,2]{1,0,7,6,5,4,3,2:T(8,128)} %bitcast.62, f32[]{:T(128)} %constant.98.clone.1), dimensions={3,5,7}, to_apply=%region_9.10 | reduce | flops 2293760 | bytes 11796484 | tf_op jit(solution)/shard_map/reduce_sum | solution.py:58
  1155.5 3.8 fusion.6
  1160.6 1.3 copy.99
  (164 shorter events, 59.9 us)
Async XLA Ops:
  0.0 41.5 %copy-start.4 = (s32[1,20]{1,0:T(1,128)S(1)}, s32[1,20]{1,0:T(1,128)}, u32[]{:S(2)}) copy-start(s32[1,20]{1,0:T(1,128)} %param.8) | copy-start | bytes 244
  0.0 41.7 %collective-permute-start.4 = (s32[1,20]{1,0:T(1,128)}, s32[1,20]{1,0:T(1,128)S(1)}, u32[]{:S(2)}, u32[]{:S(2)}) collective-permute-start(s32[1,20]{1,0:T(1,128)} %param.8), channel_id=1, source_target_pairs={{0,16},{16,32},{32,48},{48,64},{64,80},{80,96},{96,112},{1,17},{17... | collective-permute-start | bytes 248 | tf_op jit(solution)/shard_map/ppermute | solution.py:14
  5.4 36.3 %collective-permute-start.5 = (s32[1,20]{1,0:T(1,128)}, s32[1,20]{1,0:T(1,128)S(1)}, u32[]{:S(2)}, u32[]{:S(2)}) collective-permute-start(s32[1,20]{1,0:T(1,128)} %param.8), channel_id=1, source_target_pairs={{16,0},{32,16},{48,32},{64,48},{80,64},{96,80},{112,96},{17,1},{33... | collective-permute-start | bytes 248 | tf_op jit(solution)/shard_map/ppermute | solution.py:15
  34.9 4.0 copy-start.1
  38.9 11.4 collective-permute-start
  40.2 10.0 collective-permute-start.1
  41.8 4.2 collective-permute-start.6
  44.7 5.5 collective-permute-start.7
  56.1 4.1 copy-start
  60.7 86.6 %collective-permute-start.2 = (bf16[34,64,8]{1,2,0:T(8,128)(2,1)S(1)}, bf16[34,64,8]{1,2,0:T(8,128)(2,1)S(1)}, u32[]{:S(2)}, u32[]{:S(2)}) collective-permute-start(bf16[34,64,8]{1,2,0:T(8,128)(2,1)S(1)} %copy.100), channel_id=1, source_target_pairs={{0,1},{1,2},{2,3},{3,4},{4,5},{5,6},{6,7},{7,8},{8,9},{9,10},{10,1... | collective-permute-start | bytes 104456 | tf_op jit(solution)/shard_map/ppermute | solution.py:14
  62.9 84.5 %collective-permute-start.3 = (bf16[34,64,8]{1,2,0:T(8,128)(2,1)S(1)}, bf16[34,64,8]{1,2,0:T(8,128)(2,1)S(1)}, u32[]{:S(2)}, u32[]{:S(2)}) collective-permute-start(bf16[34,64,8]{1,2,0:T(8,128)(2,1)S(1)} %copy.101), channel_id=1, source_target_pairs={{1,0},{2,1},{3,2},{4,3},{5,4},{6,5},{7,6},{8,7},{9,8},{10,9},{11,1... | collective-permute-start | bytes 104456 | tf_op jit(solution)/shard_map/ppermute | solution.py:15
  110.8 158.3 %all-to-all-start.1 = ((bf16[32,3,3]{2,1,0:T(4,128)(2,1)}), bf16[32,3,3]{2,1,0:T(4,128)(2,1)S(1)}, u32[]{:S(2)}, u32[]{:S(2)}) async-start(bf16[32,3,3]{2,1,0:T(4,128)(2,1)} %convert_element_type.55), calls=%async_computation.1 | async-start | bytes 65536 | tf_op jit(solution)/shard_map/all_to_all | solution.py:120
  269.1 7.5 copy-start.3
  269.1 7.7 copy-start.2
  269.1 8.1 copy-start.5
  269.1 674.5 %all-to-all-start = ((bf16[32,34,64,144]{3,2,1,0:T(8,128)(2,1)}), bf16[32,34,64,144]{3,2,1,0:T(8,128)(2,1)}, u32[]{:S(2)}, u32[]{:S(2)}) async-start(bf16[32,34,64,144]{3,2,1,0:T(8,128)(2,1)} %copy.89), calls=%async_computation | async-start | bytes 71303168 | tf_op jit(solution)/shard_map/all_to_all | solution.py:119
  978.9 29.9 %copy-start.6 = (f32[64]{0:T(128)S(1)}, f32[64]{0:T(128)}, u32[]{:S(2)}) copy-start(f32[64]{0:T(128)} %param.11) | copy-start | bytes 772
  978.9 29.9 %copy-start.7 = (f32[64]{0:T(128)S(1)}, f32[64]{0:T(128)}, u32[]{:S(2)}) copy-start(f32[64]{0:T(128)} %param.13) | copy-start | bytes 772
where the time goes:
time: 1170 us; the launch traced here: 1160 us
  waiting for transfers between devices  666 us (57%)
  local copies, waits for them, and re-layouts  208 us (18%)
  matrix products  162 us (14%)
  other arithmetic  78.5 us (7%)
  starting transfers between devices  29.1 us (2%)
  blocking collectives  18 us (2%)
    all_to_all x1, waiting for transfers between devices, per_device(): lax.all_to_all(picked, 'xy', split_axis=0, concat_axis=0, tiled=True)  662 us
    conv_general_dilated x1, matrix products, conv_chain(): lax.conv_general_dilated(hidden, kernel_two, (1, 1, 1), ((0, 0), (0, 0),...  131 us
    gather x2, local copies, waits for them, and re-layouts, cut_brick(): lax.dynamic_slice_in_dim(full_rims, column_index * brick_span, (brick_sid...  91.2 us
    gather x96, local copies, waits for them, and re-layouts  45.9 us
    concatenate x4, other arithmetic, padded(): value = jnp.concatenate([before, value, after], axis=dim)  36.4 us
    conv_general_dilated x1, matrix products, conv_chain(): lax.conv_general_dilated(extended, kernel_one, (1, 1, 1), ((0, 0), (0, 0)...  29.9 us
    concatenate x1, local copies, waits for them, and re-layouts, padded(): value = jnp.concatenate([before, value, after], axis=dim)  27.6 us
    gather x2, local copies, waits for them, and re-layouts, per_device(): chosen_bricks = jnp.take(arrived, arrival, axis=0)  26.8 us
  transfers between devices with their start and end apart: 10, of which 2 were waited for; matrix products, arithmetic and copies ran while one was open for 19% of the time, Pallas kernels for 0%

commit v1 on v0

v1 whole, which is shorter than its diff:
```python
import functools

import jax
import jax.numpy as jnp
from jax import lax
from jax.experimental import pallas as pl
from jax.experimental.pallas import tpu as pltpu
from jax.sharding import PartitionSpec as P

SEG = 16
HALF = 64


def shift(value, axis, step):
    peers = lax.axis_size(axis)
    pairs = [(i, i + step) for i in range(peers) if 0 <= i + step < peers]
    return lax.ppermute(value, axis, pairs)


EMPTY = 100.0
BREAKS = (-2, 0, 8, 16, 24, 32, 40, 42)


def span(t):
    return max(i for i, start in enumerate(BREAKS) if start <= t)


FRONT, PAD = 16, 4


class Spread:
    def __init__(self, work, steps):
        self.work, self.steps, self.done = list(work), steps, 0

    def step(self):
        self.done += 1
        for piece in self.work[
            len(self.work) * (self.done - 1) // self.steps:len(self.work) * self.done // self.steps
        ]:
            piece()


def mix(one, two):
    places = [((i + 0.5) / len(part), piece) for part in (one, two) for i, piece in enumerate(part)]
    return [piece for _, piece in sorted(places, key=lambda entry: entry[0])]


def features_kernel(
    order_ref, near_ref, far1_ref, far2_ref, far3_ref, first_ref, vol0_ref, vol1_ref, vol2_ref, vol3_ref, below_ref, above_ref,
    left_ref, right_ref, w1_ref, b1_ref, w2_ref, b2_ref,
    sent_ref, arrival_ref, flip, taps, hidden, masks, pooled, staged, slots, sems,
):
    group = pl.program_id(0)
    last = group == pl.num_programs(0) - 1
    chans, lanes = vol0_ref.shape[1], vol0_ref.shape[2]
    columns = lanes // 128
    runs = lanes // (4 * SEG)
    low = lax.broadcasted_iota(jnp.int32, (SEG, 128), 1) < HALF
    low8 = lax.broadcasted_iota(jnp.int32, (8, 128), 1) < HALF
    body_rows = runs * SEG
    first_rows = body_rows + 2 * SEG

    own = lax.axis_index("xy")
    groups = 4 * near_ref.shape[0]
    fars = (near_ref, far1_ref, far2_ref, far3_ref)

    def route():
        counts = []
        for k in range(groups):
            marks = fars[k // 4]
            count = marks[k % 4, 0]
            for j in range(1, columns):
                count = count + marks[k % 4, j]
            counts.append(count)
        start = jnp.int32(0)
        for k in range(1, groups):
            start = start + jnp.where((own ^ k) < own, counts[k], 0)
        rank = jnp.int32(0)
        for j in range(columns):
            full = near_ref[0, j]
            to = order_ref[0, (start + rank) & (groups - 1)]
            slots[j] = jnp.where(full > 0, 2 * to + (rank >= groups).astype(jnp.int32), -1)
            rank = rank + full
        label = jnp.int32(0)
        for i in range(groups):
            label = label + jnp.where(order_ref[0, i] == own, i, 0)
        for k in range(groups):
            begin = jnp.int32(0)
            for m in range(groups):
                if m != k:
                    begin = begin + jnp.where((own ^ m) < (own ^ k), counts[m], 0)
            ahead = (label - begin) & (groups - 1)
            for second in range(2):
                at = ahead + groups * second

                @pl.when(at < counts[k])
                def _():
                    arrival_ref[(begin + at) // groups] = 2 * (own ^ k) + second

    def turn_pieces(source, at_rim):
        def piece(j):
            block = jnp.concatenate([source(0, 128 * j), source(1, 128 * j)], axis=0)
            block = block.astype(jnp.float32).T
            start = 128 * j
            while start < 128 * j + 128:
                s = start // (4 * runs)
                stop = min(128 * j + 128, 4 * runs * (s + 1))
                to = FRONT + PAD * s + start
                flip[to:to + stop - start, :] = block[start - 128 * j:stop - 128 * j]
                start = stop

        def sides():
            flip[FRONT - PAD - 8:FRONT - PAD, :] = left_ref[at_rim].astype(jnp.float32)
            end = FRONT + SEG * (4 * runs + PAD)
            flip[end:end + 8, :] = right_ref[at_rim].astype(jnp.float32)

        return [sides] + [functools.partial(piece, j) for j in range(columns)]

    def turn(source, at_rim):
        for piece in turn_pieces(source, at_rim):
            piece()

    def row_tiles(t):
        start = FRONT + 4 * t + (-PAD if t < 0 else PAD if t >= runs else 0)
        rows = [flip[pl.ds(start + x, SEG, stride=4 * runs + PAD), :] for x in range(4)]
        turned = [pltpu.roll(row, HALF, 1) for row in rows]
        return [
            [
                jnp.where(low, rows[2 * h], turned[2 * h + 1]).astype(jnp.bfloat16)
                for h in range(2)
            ],
            [
                jnp.where(low, turned[2 * h], rows[2 * h + 1]).astype(jnp.bfloat16)
                for h in range(2)
            ],
        ]

    def store_taps(slot, layer, t, tiles, keep):
        for h in range(2):
            taps[slot, layer, SEG * (t + 2):SEG * (t + 3), 128 * h:128 * h + 128] = (
                tiles[layer][h] * keep
            )

    def row_pieces(slot, kinds):
        def piece(t):
            tiles = row_tiles(t)
            for layer in range(2):
                store_taps(slot, layer, t, tiles, masks[kinds[layer], span(t)])

        return [functools.partial(piece, t) for t in range(-2, runs + 2)]

    def first_dots(slot, work=()):
        total = None
        work = Spread(work, 3)
        for b in range(3):
            part = jnp.dot(
                taps[slot, :, SEG * b:SEG * b + first_rows, :].reshape(2 * first_rows, 256),
                w1_ref[b], preferred_element_type=jnp.float32,
            )
            total = part if total is None else total + part
            work.step()
        return total

    def first_pieces(total, kinds, places):
        def piece(layer, lo, hi, keep):
            at = layer * first_rows
            act = total[at + SEG * lo:at + SEG * hi]
            act = jnp.maximum(act + b1_ref[...], 0.0).astype(jnp.bfloat16)
            act = act.reshape(hi - lo, SEG, 256)
            for h in range(2):
                hidden[places[layer], SEG * lo:SEG * hi, 128 * h:128 * h + 128] = (
                    act[:, :, 128 * h:128 * h + 128] * keep()[None]
                ).reshape(SEG * (hi - lo), 128)

        made = []
        for layer in range(2):
            for i in range(len(BREAKS) - 1):
                lo, hi = max(BREAKS[i], -1) + 1, min(BREAKS[i + 1], runs + 1) + 1
                keep = functools.partial(lambda kind, i: masks[kind, i], kinds[layer], i)
                made.append(functools.partial(piece, layer, lo, hi, keep))
        return made

    def first_conv(slot, kinds, places):
        for piece in first_pieces(first_dots(slot), kinds, places):
            piece()

    def second_dots(places, ends, early, late):
        total = None
        early, late = Spread(early, 6), Spread(late, 9)
        for a in range(3):
            for b in range(3):
                rows = slice(SEG * b, SEG * b + body_rows)
                later = hidden[places[a + 1], rows, :]
                if ends and a == 2:
                    later = jnp.where(last, hidden[8, rows, :], later)
                part = jnp.dot(
                    jnp.concatenate([hidden[places[a], rows, :], later], axis=0),
                    w2_ref[3 * a + b], preferred_element_type=jnp.float32,
                )
                total = part if total is None else total + part
                if a < 2:
                    early.step()
                late.step()
        return total

    def second_pieces(slot, total):
        def piece(u):
            summed = None
            for at in (2 * u, 2 * u + 1, runs + 2 * u, runs + 2 * u + 1):
                part = jnp.maximum(total[SEG * at:SEG * at + SEG] + b2_ref[...], 0.0)
                summed = part if summed is None else summed + part
            for x2 in range(2):
                half = summed[:, 128 * x2:128 * x2 + 128]
                half = (half + pltpu.roll(half, HALF, 1)) * 0.125
                both = jnp.where(low8, half[0:8], half[8:16])
                pooled[slot, pl.ds(2 * u + x2, 8, stride=runs), :] = both

        return [functools.partial(piece, u) for u in range(runs // 2)]

    def of(ref):
        return lambda layer, at: ref[layer, :, at:at + 128]

    @pl.when(group == 0)
    def _():
        row = lax.broadcasted_iota(jnp.int32, (SEG, 128), 0)
        one, zero = jnp.ones((SEG, 128), jnp.bfloat16), jnp.zeros((SEG, 128), jnp.bfloat16)
        has = [
            lax.axis_index("gz") > 0, lax.axis_index("gz") < lax.axis_size("gz") - 1,
            own > 0, own < groups - 1,
        ]
        route()

        def inside(i):
            keep = None
            if BREAKS[i] < 0:
                keep = has[2] | (row > 0)
            elif BREAKS[i] >= runs:
                keep = has[3] | (row < SEG - 1)
            return keep

        turn(lambda layer, at: (below_ref, above_ref)[layer][0, :, at:at + 128], 0)
        for t in range(-2, runs + 2):
            tiles = row_tiles(t)
            for layer in range(2):
                i = span(t)
                if t == BREAKS[i]:
                    keep = (tiles[layer][0].astype(jnp.float32) < 50.0) & has[layer]
                    if inside(i) is not None:
                        keep = keep & inside(i)
                    masks[layer, i] = jnp.where(keep, 1.0, 0.0).astype(jnp.bfloat16)
                store_taps(0, layer, t, tiles, masks[layer, i])
        first_conv(0, [0, 1], [7, 8])

        turn(of(first_ref), 1)
        for i in range(len(BREAKS) - 1):
            t = BREAKS[i]
            keep = jnp.zeros((SEG, 128), jnp.float32)
            for s in range(SEG):
                column = (runs * s + t) // 32
                if 0 <= column < columns:
                    keep = jnp.where(row == s, near_ref[0, column].astype(jnp.float32), keep)
            keep = keep > 0.5
            seen = row_tiles(t)[0][0].astype(jnp.float32) < 50.0
            if t < 0:
                keep = keep | ((row == 0) & seen & has[2])
            elif t >= runs:
                keep = keep | ((row == SEG - 1) & seen & has[3])
            masks[2, i] = jnp.where(keep, 1.0, 0.0).astype(jnp.bfloat16)
        for t in range(-2, runs + 2):
            tiles = row_tiles(t)
            for layer in range(2):
                store_taps(0, layer, t, tiles, masks[2, span(t)])
        first_conv(0, [2, 2], [0, 1])
        turn(lambda layer, at: first_ref[2 + layer, :, at:at + 128], 2)
        for piece in row_pieces(1, [2, 2]):
            piece()

    top = left_ref.shape[0] - 1
    pooling = []
    for i, ref in enumerate((vol0_ref, vol1_ref, vol2_ref, vol3_ref)):
        nxt = 2 * ((i + 1) % 4)
        turning = turn_pieces(of(ref), jnp.minimum(4 * group + i + 3, top))
        total = first_dots((i + 1) % 2, mix(pooling, turning))
        total = second_dots(
            [2 * ((i + 3) % 4) + 1, 2 * i, 2 * i + 1, nxt], i == 3,
            first_pieces(total, [2, 2], [nxt, nxt + 1]), row_pieces(i % 2, [2, 2]),
        )
        pooling = second_pieces(i, total)
    for piece in pooling:
        piece()

    def leave(part, j):
        at = pl.multiple_of(part * 128, 128)
        return pltpu.make_async_copy(
            staged.at[part, j], sent_ref.at[jnp.maximum(slots[j], 0), :, pl.ds(at, 128)],
            sems.at[j],
        )

    for j in range(columns // 2):
        block = pooled[:, 32 * j:32 * j + 32, :].reshape(128, 128).T.astype(jnp.bfloat16)
        staged[group, j] = block[0:chans]
        staged[group, j + columns // 2] = block[chans:]
    for j in range(columns):
        @pl.when(slots[j] >= 0)
        def _():
            leave(group, j).start()

    @pl.when(last)
    def _():
        for j in range(columns):
            @pl.when(slots[j] >= 0)
            def _():
                for part in range(4):
                    leave(part, j).wait()


def local_features(order, near, far, volume, below, above, left, right, w1, b1, w2, b2):
    layers, chans, lanes = volume.shape
    columns = lanes // 128
    runs = lanes // (4 * SEG)
    pairs = layers // 2
    groups = 4 * near.shape[0]

    def whole(array):
        return pl.BlockSpec(array.shape, lambda g: (0,) * array.ndim)

    def pair(i):
        return pl.BlockSpec(
            (2, chans, lanes), lambda g: (jnp.minimum(4 * g + i + 2, pairs - 1), 0, 0)
        )

    scalar = pl.BlockSpec(memory_space=pltpu.SMEM)
    rows = runs * SEG
    return pl.pallas_call(
        features_kernel,
        grid=(pairs // 4,),
        in_specs=[
            scalar, scalar, scalar, scalar, scalar,
            pl.BlockSpec((4, chans, lanes), lambda g: (0, 0, 0)),
            pair(0), pair(1), pair(2), pair(3),
            whole(below), whole(above), whole(left), whole(right),
            whole(w1), whole(b1), whole(w2), whole(b2),
        ],
        out_specs=[pl.BlockSpec(memory_space=pl.ANY), scalar],
        out_shape=[
            jax.ShapeDtypeStruct((2 * groups, chans, 512), jnp.bfloat16),
            jax.ShapeDtypeStruct((columns // 2,), jnp.int32),
        ],
        scratch_shapes=[
            pltpu.VMEM((FRONT + SEG * (4 * runs + PAD) + 8, 128), jnp.float32),
            pltpu.VMEM((2, 2, rows + 4 * SEG, 256), jnp.bfloat16),
            pltpu.VMEM((9, rows + 2 * SEG, 256), jnp.bfloat16),
            pltpu.VMEM((3, len(BREAKS) - 1, SEG, 128), jnp.bfloat16),
            pltpu.VMEM((4, lanes // 8, 128), jnp.float32),
            pltpu.VMEM((4, columns, chans, 128), jnp.bfloat16),
            pltpu.SMEM((columns,), jnp.int32),
            pltpu.SemaphoreType.DMA((columns,)),
        ],
        compiler_params=pltpu.CompilerParams(vmem_limit_bytes=48 << 20),
        cost_estimate=pl.CostEstimate(
            flops=33_000_000_000, bytes_accessed=16_000_000, transcendentals=0
        ),
    )(order, near, *far, volume, volume, volume, volume, volume, below, above, left, right,
      w1, b1, w2, b2)


def banded(weight, taps):
    chans = weight.shape[0]
    parts = weight.reshape(chans, taps, 3, chans).transpose(1, 2, 3, 0)
    blank = jnp.zeros_like(parts[:, 0])
    rows = [
        jnp.concatenate(
            [parts[:, x - to + 1] if 0 <= x - to + 1 < 3 else blank for to in range(4)], axis=2
        )
        for x in range(4)
    ]
    return jnp.concatenate(rows, axis=1)


def per_device(volume, occupancy, device_order, weight_one, bias_one, weight_two, bias_two):
    layers, chans, lanes = volume.shape
    columns = occupancy.shape[1]
    groups = lax.axis_size("xy")
    tissue_row = occupancy[0]

    def swap(value, k):
        return lax.ppermute(value, "xy", [(i, i ^ k) for i in range(groups)])

    near = jnp.concatenate([occupancy] + [swap(occupancy, k) for k in (1, 2, 3)], axis=0)

    full = jnp.repeat(tissue_row, lanes // columns)[None, None, :] > 0
    empty = jnp.asarray(EMPTY, volume.dtype)
    below = shift(jnp.where(full, volume[layers - 1:], empty), "gz", 1)
    above = shift(jnp.where(full, volume[:1], empty), "gz", -1)

    def edge(start, mark):
        def turned(rows):
            pairs = rows.reshape(-1, 2, chans, 8).transpose(0, 3, 1, 2)
            return pairs.reshape(-1, 8, 2 * chans)

        own = jnp.where(mark > 0, volume[:, :, start:start + 8], empty)
        ends = [below[:, :, start:start + 8], above[:, :, start:start + 8]]
        return jnp.concatenate([turned(jnp.concatenate(ends, axis=0)), turned(own)], axis=0)

    left = shift(edge(lanes - 8, tissue_row[columns - 1]), "xy", 1)
    right = shift(edge(0, tissue_row[0]), "xy", -1)
    far = [swap(near, 4 * k) for k in (1, 2, 3)]

    w1, w2 = banded(weight_one, 3), banded(weight_two, 9)
    b1, b2 = jnp.tile(bias_one, 4)[None], jnp.tile(bias_two, 4)[None]
    sent, arrival = local_features(
        device_order, near, far, volume, below, above, left, right, w1, b1, w2, b2
    )
    arrived = lax.all_to_all(sent, "xy", split_axis=0, concat_axis=0, tiled=True)
    return jnp.take(arrived, arrival, axis=0, mode="clip")


def solution(mesh):
    in_specs = (P("gz", None, "xy"), P("gz", "xy"), P("gz", None), P(), P(), P(), P())
    out_specs = P(("gz", "xy"), None, None)
    return jax.shard_map(
        per_device, mesh=mesh, in_specs=in_specs, out_specs=out_specs, check_vma=False
    )
```

time: 1170 us -> 120 us (0.10)
  waiting for transfers between devices: 666 us -> 32.9 us
  local copies, waits for them, and re-layouts: 208 us -> 7.92 us
  matrix products: 162 us -> 0 us
  other arithmetic: 78.5 us -> 6.78 us
  Pallas kernels: 0 us -> 45.5 us
  blocking collectives: 18 us -> 0 us
    all_to_all x2 -> x1, waiting for transfers between devices: 662 us -> 29 us  [per_device(): lax.all_to_all(sent, 'xy', split_axis=0, concat_axis=0, tiled=True)]
    gather x101 -> x1, local copies, waits for them, and re-layouts: 165 us -> 1.46 us  [per_device(): return jnp.take(arrived, arrival, axis=0, mode='clip')]
    conv_general_dilated x2 -> x0, matrix products: 161 us -> none  [the longest x1 131 us: conv_chain(): lax.conv_general_dilated(hidden, kernel_two, (1, 1, 1), ((0, 0), (0, 0),...]
    pallas_call x0 -> x1, Pallas kernels: none -> 45.5 us  [local_features(): pl.pallas_call(features_kernel, grid=(pairs // 4,), in_specs=[scalar, sca...]
    concatenate x4 -> x5, other arithmetic: 36.4 us -> 3.5 us  [the longest x2 3.47 us: banded(): return jnp.concatenate(rows, axis=1)]
    concatenate x2 -> x0, local copies, waits for them, and re-layouts: 27.6 us -> none  [the longest x1 27.6 us: padded(): value = jnp.concatenate([before, value, after], axis=dim)]
    reduce_sum x8 -> x0, other arithmetic: 19.2 us -> none  [the longest x1 15.3 us: conv_chain(): pooled = jnp.mean(second_act, axis=(3, 5, 7))]
    unnamed x1 -> x0, blocking collectives: 18 us -> none
  transfers between devices with their start and end apart: 10 -> 11, of which waited for: 2 -> 3; matrix products, arithmetic and copies ran while one was open for 19% -> 11% of each run, Pallas kernels for 0% -> 0%
where the time goes in v1:
time: 120 us
  Pallas kernels  45.5 us (38%)
  waiting for transfers between devices  32.9 us (27%)
  starting transfers between devices  25.2 us (21%)
  local copies, waits for them, and re-layouts  7.92 us (7%)
  other arithmetic  6.78 us (6%)
  between operations  1.57 us (1%)
    pallas_call x1, Pallas kernels, local_features(): pl.pallas_call(features_kernel, grid=(pairs // 4,), in_specs=[scalar, sca...  45.5 us
    all_to_all x1, waiting for transfers between devices, per_device(): lax.all_to_all(sent, 'xy', split_axis=0, concat_axis=0, tiled=True)  29 us
    ppermute x6, starting transfers between devices, swap(): return lax.ppermute(value, 'xy', [(i, i ^ k) for i in range(groups)])  12.6 us
    ppermute x4, starting transfers between devices, shift(): return lax.ppermute(value, axis, pairs)  8.7 us
    ppermute x6, waiting for transfers between devices, swap(): return lax.ppermute(value, 'xy', [(i, i ^ k) for i in range(groups)])  3.97 us
    all_to_all x1, starting transfers between devices, per_device(): lax.all_to_all(sent, 'xy', split_axis=0, concat_axis=0, tiled=True)  3.93 us
    concatenate x2, other arithmetic, banded(): return jnp.concatenate(rows, axis=1)  3.47 us
    reshape x3, local copies, waits for them, and re-layouts, banded(): parts = weight.reshape(chans, taps, 3, chans).transpose(1, 2, 3, 0)  2.45 us
  transfers between devices with their start and end apart: 11, of which 3 were waited for; matrix products, arithmetic and copies ran while one was open for 11% of the time, Pallas kernels for 0%

profile of v1, /device:TPU:0, one launch (start us, length us, event | category | flops | bytes accessed | tf_op | source)
XLA Modules:
  0.0 119.9 jit_solution(3613773170193311883)
XLA Ops:
  0.0 4.1 %collective-permute-start.2 = (s32[1,20]{1,0:T(1,128)}, s32[1,20]{1,0:T(1,128)S(1)}, u32[]{:S(2)}, u32[]{:S(2)}) collective-permute-start(s32[1,20]{1,0:T(1,128)} %param.8), channel_id=1, source_target_pairs={{0,3},{1,2},{2,1},{3,0},{4,7},{5,6},{6,5},{7,4},{8,11},{9,10},{10,... | collective-permute-start | bytes 248 | tf_op jit(solution)/shard_map/ppermute | solution.py:387
  4.1 0.9 collective-permute-start
  5.0 0.7 compare_bitcast_fusion
  5.8 1.1 slice_select_fusion.2
  6.9 1.3 %collective-permute-start.7 = (bf16[1,64,2560]{2,1,0:T(8,128)(2,1)S(1)}, bf16[1,64,2560]{2,1,0:T(8,128)(2,1)S(1)}, u32[]{:S(2)}, u32[]{:S(2)}) collective-permute-start(bf16[1,64,2560]{2,1,0:T(8,128)(2,1)S(1)} %get-tuple-element.9), channel_id=1, source_target_pairs={{16,0},{32,16},{48,32},{64,48},{80,64},{96,80},{112,96},{17,1},{33... | collective-permute-start | bytes 983048 | tf_op jit(solution)/shard_map/ppermute | solution.py:17
  8.2 3.1 %collective-permute-start.6 = (bf16[1,64,2560]{2,1,0:T(8,128)(2,1)S(1)}, bf16[1,64,2560]{2,1,0:T(8,128)(2,1)S(1)}, u32[]{:S(2)}, u32[]{:S(2)}) collective-permute-start(bf16[1,64,2560]{2,1,0:T(8,128)(2,1)S(1)} %get-tuple-element.10), channel_id=1, source_target_pairs={{0,16},{16,32},{32,48},{48,64},{64,80},{80,96},{96,112},{1,17},{17... | collective-permute-start | bytes 983048 | tf_op jit(solution)/shard_map/ppermute | solution.py:17
  11.2 1.3 %fusion.2 = (s32[1,1]{1,0:T(1,128)}, s32[1,1]{1,0:T(1,128)}) fusion(s32[1,20]{1,0:T(1,128)} %param.8), kind=kLoop, calls=%fused_computation.24 | loop fusion | bytes 16 | tf_op jit(solution)/shard_map/slice | solution.py:406
  13.9 1.0 copy.27
  14.9 1.5 %reshape.62 = bf16[64,9,3,64]{3,2,1,0:T(4,128)(2,1)S(1)} reshape(bf16[64,1728]{1,0:T(8,128)(2,1)} %param.12) | data formatting | bytes 442368 | tf_op jit(solution)/shard_map/reshape | solution.py:369
  16.5 0.9 copy.29
  17.4 1.4 %slice_select_fusion = (bf16[32,64,8]{2,1,0:T(8,128)(2,1)S(1)}, bf16[32,64,8]{2,1,0:T(8,128)(2,1)S(1)}) fusion(bf16[32,64,2560]{2,1,0:T(8,128)(2,1)} %vol3_ref.1, pred[]{:T(512)} %bitcast.9, pred[]{:T(512)} %bitcast.4), kind=kLoop, calls=%fused_computation.2 | loop fusion | flops 32768 | bytes 131074 | tf_op jit(solution)/shard_map/jit(_where)/select_n | solution.py:401
  18.8 0.2 copy.26
  19.1 0.1 reshape.60
  19.2 0.2 copy.22
  19.4 0.1 reshape.56
  19.6 3.3 %maximum_maximum_fusion.w2_ref = bf16[9,256,256]{2,1,0:T(8,128)(2,1)S(1)} fusion(bf16[9,64,64]{2,1,0:T(8,128)(2,1)S(1)} %get-tuple-element.15, bf16[9,64,64]{2,1,0:T(8,128)(2,1)S(1)} %get-tuple-element.14, bf16[9,64,128]{2,1,0:T(8,128)(2,1)S(1)} %broadcast.21, bf16[9,64,64]{2,1,0:T(8,128)(2,1)S(1)} %get-tuple-element.13, ...), kind=kLoop, calls=%fused_computation.1 | loop fusion | flops 16515072 | bytes 1622016 | tf_op jit(solution)/shard_map/concatenate | solution.py:377
  22.9 0.2 maximum_maximum_fusion.1.w1_ref
  23.4 0.1 fusion
  23.6 0.1 reshape.58
  23.8 3.1 %collective-permute-start.8 = (bf16[17,8,128]{2,1,0:T(8,128)(2,1)S(1)}, bf16[17,8,128]{2,1,0:T(8,128)(2,1)S(1)}, u32[]{:S(2)}, u32[]{:S(2)}) collective-permute-start(bf16[17,8,128]{2,1,0:T(8,128)(2,1)S(1)} %pad_maximum_fusion), channel_id=1, source_target_pairs={{0,1},{1,2},{2,3},{3,4},{4,5},{5,6},{6,7},{7,8},{8,9},{9,10},{10,1... | collective-permute-start | bytes 104456 | tf_op jit(solution)/shard_map/ppermute | solution.py:17
  26.9 1.3 %collective-permute-start.9 = (bf16[17,8,128]{2,1,0:T(8,128)(2,1)S(1)}, bf16[17,8,128]{2,1,0:T(8,128)(2,1)S(1)}, u32[]{:S(2)}, u32[]{:S(2)}) collective-permute-start(bf16[17,8,128]{2,1,0:T(8,128)(2,1)S(1)} %pad_maximum_fusion.1), channel_id=1, source_target_pairs={{1,0},{2,1},{3,2},{4,3},{5,4},{6,5},{7,6},{8,7},{9,8},{10,9},{11,1... | collective-permute-start | bytes 104456 | tf_op jit(solution)/shard_map/ppermute | solution.py:17
  28.3 6.7 %collective-permute-start.5 = (s32[4,20]{1,0:T(4,128)S(1)}, s32[4,20]{1,0:T(4,128)S(1)}, u32[]{:S(2)}, u32[]{:S(2)}) collective-permute-start(s32[4,20]{1,0:T(4,128)S(1)} %pad_add_fusion.near_ref), channel_id=1, source_target_pairs={{0,12},{1,13},{2,14},{3,15},{4,8},{5,9},{6,10},{7,11},{8,4},{9,5},... | collective-permute-start | bytes 968 | tf_op jit(solution)/shard_map/ppermute | solution.py:387
  35.0 0.6 collective-permute-start.4
  35.6 0.3 collective-permute-start.3
  35.9 0.1 broadcast_in_dim_tile.6.b1_ref
  36.0 0.1 broadcast_in_dim_tile.7.b2_ref
  36.1 0.4 collective-permute-done.5.far3_ref
  36.5 3.5 %collective-permute-done.4.far2_ref = s32[4,20]{1,0:T(4,128)S(1)} collective-permute-done((s32[4,20]{1,0:T(4,128)S(1)}, s32[4,20]{1,0:T(4,128)S(1)}, u32[]{:S(2)}, u32[]{:S(2)}) %collective-permute-start.4) | collective-permute-done | bytes 352 | tf_op jit(solution)/shard_map/ppermute | solution.py:387
  40.1 45.5 %shard_map.73 = (bf16[32,64,512]{2,1,0:T(8,128)(2,1)}, s32[10]{0:T(128)S(1)}) custom-call(s32[1,16]{1,0:T(1,128)S(1)} %copy-done, s32[4,20]{1,0:T(4,128)S(1)} %pad_add_fusion.near_ref, s32[4,20]{1,0:T(4,128)S(1)} %collective-permute-done.3.far1_ref, s32[4,20]{1,0:T(4,128)S(1)} %collective-permute-done.4.far2_ref, ...), custom_call_target="tpu_custom_call" | custom-call | flops 32999999488 | bytes 16000000 | tf_op jit(solution)/shard_map/pallas_call | solution.py:334
  85.6 3.9 %all-to-all-start = ((bf16[32,64,512]{2,1,0:T(8,128)(2,1)}), bf16[32,64,512]{2,1,0:T(8,128)(2,1)S(1)}, u32[]{:S(2)}, u32[]{:S(2)}) async-start(bf16[32,64,512]{2,1,0:T(8,128)(2,1)} %get-tuple-element.7), calls=%async_computation | async-start | bytes 4194304 | tf_op jit(solution)/shard_map/all_to_all | solution.py:414
  89.5 29.0 %all-to-all-done = bf16[32,64,512]{2,1,0:T(8,128)(2,1)S(1)} async-done(((bf16[32,64,512]{2,1,0:T(8,128)(2,1)}), bf16[32,64,512]{2,1,0:T(8,128)(2,1)S(1)}, u32[]{:S(2)}, u32[]{:S(2)}) %all-to-all-start) | async-done | bytes 2097184 | tf_op jit(solution)/shard_map/all_to_all | solution.py:414
  118.5 1.5 %gather_fusion = bf16[10,64,512]{2,1,0:T(8,128)(2,1)} fusion(bf16[32,64,512]{2,1,0:T(8,128)(2,1)S(1)} %all-to-all-done, s32[1024]{0:T(1024)S(1)} %pad_clamp_fusion), kind=kCustom, calls=%fused_computation | custom fusion | bytes 1310760 | tf_op jit(solution)/shard_map/jit(_take)/gather | solution.py:415
  (41 shorter events, 0.8 us)
Async XLA Ops:
  0.0 28.2 %collective-permute-start.2 = (s32[1,20]{1,0:T(1,128)}, s32[1,20]{1,0:T(1,128)S(1)}, u32[]{:S(2)}, u32[]{:S(2)}) collective-permute-start(s32[1,20]{1,0:T(1,128)} %param.8), channel_id=1, source_target_pairs={{0,3},{1,2},{2,1},{3,0},{4,7},{5,6},{6,5},{7,4},{8,11},{9,10},{10,... | collective-permute-start | bytes 248 | tf_op jit(solution)/shard_map/ppermute | solution.py:387
  4.1 24.1 %collective-permute-start.1 = (s32[1,20]{1,0:T(1,128)}, s32[1,20]{1,0:T(1,128)S(1)}, u32[]{:S(2)}, u32[]{:S(2)}) collective-permute-start(s32[1,20]{1,0:T(1,128)} %param.8), channel_id=1, source_target_pairs={{0,2},{1,3},{2,0},{3,1},{4,6},{5,7},{6,4},{7,5},{8,10},{9,11},{10,... | collective-permute-start | bytes 248 | tf_op jit(solution)/shard_map/ppermute | solution.py:387
  4.1 24.1 %collective-permute-start = (s32[1,20]{1,0:T(1,128)}, s32[1,20]{1,0:T(1,128)S(1)}, u32[]{:S(2)}, u32[]{:S(2)}) collective-permute-start(s32[1,20]{1,0:T(1,128)} %param.8), channel_id=1, source_target_pairs={{0,1},{1,0},{2,3},{3,2},{4,5},{5,4},{6,7},{7,6},{8,9},{9,8},{10,11... | collective-permute-start | bytes 248 | tf_op jit(solution)/shard_map/ppermute | solution.py:387
  6.9 16.2 %collective-permute-start.7 = (bf16[1,64,2560]{2,1,0:T(8,128)(2,1)S(1)}, bf16[1,64,2560]{2,1,0:T(8,128)(2,1)S(1)}, u32[]{:S(2)}, u32[]{:S(2)}) collective-permute-start(bf16[1,64,2560]{2,1,0:T(8,128)(2,1)S(1)} %get-tuple-element.9), channel_id=1, source_target_pairs={{16,0},{32,16},{48,32},{64,48},{80,64},{96,80},{112,96},{17,1},{33... | collective-permute-start | bytes 983048 | tf_op jit(solution)/shard_map/ppermute | solution.py:17
  8.2 15.2 %collective-permute-start.6 = (bf16[1,64,2560]{2,1,0:T(8,128)(2,1)S(1)}, bf16[1,64,2560]{2,1,0:T(8,128)(2,1)S(1)}, u32[]{:S(2)}, u32[]{:S(2)}) collective-permute-start(bf16[1,64,2560]{2,1,0:T(8,128)(2,1)S(1)} %get-tuple-element.10), channel_id=1, source_target_pairs={{0,16},{16,32},{32,48},{48,64},{64,80},{80,96},{96,112},{1,17},{17... | collective-permute-start | bytes 983048 | tf_op jit(solution)/shard_map/ppermute | solution.py:17
  19.0 9.2 %copy-start.1 = (s32[1,20]{1,0:T(1,128)S(1)}, s32[1,20]{1,0:T(1,128)}, u32[]{:S(2)}) copy-start(s32[1,20]{1,0:T(1,128)} %param.8) | copy-start | bytes 244
  19.1 16.9 %copy-start.2 = (f32[64]{0:T(128)S(1)}, f32[64]{0:T(128)}, u32[]{:S(2)}) copy-start(f32[64]{0:T(128)} %param.11) | copy-start | bytes 772
  19.1 16.9 %copy-start.3 = (f32[64]{0:T(128)S(1)}, f32[64]{0:T(128)}, u32[]{:S(2)}) copy-start(f32[64]{0:T(128)} %param.13) | copy-start | bytes 772
  19.1 21.0 %copy-start = (s32[1,16]{1,0:T(1,128)S(1)}, s32[1,16]{1,0:T(1,128)}, u32[]{:S(2)}) copy-start(s32[1,16]{1,0:T(1,128)} %order_ref.1) | copy-start | bytes 196
  23.8 16.2 %collective-permute-start.8 = (bf16[17,8,128]{2,1,0:T(8,128)(2,1)S(1)}, bf16[17,8,128]{2,1,0:T(8,128)(2,1)S(1)}, u32[]{:S(2)}, u32[]{:S(2)}) collective-permute-start(bf16[17,8,128]{2,1,0:T(8,128)(2,1)S(1)} %pad_maximum_fusion), channel_id=1, source_target_pairs={{0,1},{1,2},{2,3},{3,4},{4,5},{5,6},{6,7},{7,8},{8,9},{9,10},{10,1... | collective-permute-start | bytes 104456 | tf_op jit(solution)/shard_map/ppermute | solution.py:17
  26.9 13.1 %collective-permute-start.9 = (bf16[17,8,128]{2,1,0:T(8,128)(2,1)S(1)}, bf16[17,8,128]{2,1,0:T(8,128)(2,1)S(1)}, u32[]{:S(2)}, u32[]{:S(2)}) collective-permute-start(bf16[17,8,128]{2,1,0:T(8,128)(2,1)S(1)} %pad_maximum_fusion.1), channel_id=1, source_target_pairs={{1,0},{2,1},{3,2},{4,3},{5,4},{6,5},{7,6},{8,7},{9,8},{10,9},{11,1... | collective-permute-start | bytes 104456 | tf_op jit(solution)/shard_map/ppermute | solution.py:17
  28.3 8.2 %collective-permute-start.5 = (s32[4,20]{1,0:T(4,128)S(1)}, s32[4,20]{1,0:T(4,128)S(1)}, u32[]{:S(2)}, u32[]{:S(2)}) collective-permute-start(s32[4,20]{1,0:T(4,128)S(1)} %pad_add_fusion.near_ref), channel_id=1, source_target_pairs={{0,12},{1,13},{2,14},{3,15},{4,8},{5,9},{6,10},{7,11},{8,4},{9,5},... | collective-permute-start | bytes 968 | tf_op jit(solution)/shard_map/ppermute | solution.py:387
  35.0 5.1 %collective-permute-start.4 = (s32[4,20]{1,0:T(4,128)S(1)}, s32[4,20]{1,0:T(4,128)S(1)}, u32[]{:S(2)}, u32[]{:S(2)}) collective-permute-start(s32[4,20]{1,0:T(4,128)S(1)} %pad_add_fusion.near_ref), channel_id=1, source_target_pairs={{0,8},{1,9},{2,10},{3,11},{4,12},{5,13},{6,14},{7,15},{8,0},{9,1},... | collective-permute-start | bytes 968 | tf_op jit(solution)/shard_map/ppermute | solution.py:387
  35.6 4.5 %collective-permute-start.3 = (s32[4,20]{1,0:T(4,128)S(1)}, s32[4,20]{1,0:T(4,128)S(1)}, u32[]{:S(2)}, u32[]{:S(2)}) collective-permute-start(s32[4,20]{1,0:T(4,128)S(1)} %pad_add_fusion.near_ref), channel_id=1, source_target_pairs={{0,4},{1,5},{2,6},{3,7},{4,0},{5,1},{6,2},{7,3},{8,12},{9,13},{10,... | collective-permute-start | bytes 968 | tf_op jit(solution)/shard_map/ppermute | solution.py:387
  85.6 32.9 %all-to-all-start = ((bf16[32,64,512]{2,1,0:T(8,128)(2,1)}), bf16[32,64,512]{2,1,0:T(8,128)(2,1)S(1)}, u32[]{:S(2)}, u32[]{:S(2)}) async-start(bf16[32,64,512]{2,1,0:T(8,128)(2,1)} %get-tuple-element.7), calls=%async_computation | async-start | bytes 4194304 | tf_op jit(solution)/shard_map/all_to_all | solution.py:414

commit v2 on v1

--- a/solution.py
+++ b/solution.py
@@ -45,10 +45,68 @@
     return [piece for _, piece in sorted(places, key=lambda entry: entry[0])]
 
 
+def counted(marks):
+    counts = []
+    for ref in marks:
+        for row in range(ref.shape[0]):
+            count = ref[row, 0]
+            for j in range(1, ref.shape[1]):
+                count = count + ref[row, j]
+            counts.append(count)
+    return counts
+
+
+def arrival_kernel(order_ref, near_ref, far1_ref, far2_ref, far3_ref, arrival_ref):
+    own = lax.axis_index("xy")
+    counts = counted((near_ref, far1_ref, far2_ref, far3_ref))
+    groups = len(counts)
+    label = jnp.int32(0)
+    for i in range(groups):
+        label = label + jnp.where(order_ref[0, i] == own, i, 0)
+    for k in range(groups):
+        begin = jnp.int32(0)
+        for m in range(groups):
+            if m != k:
+                begin = begin + jnp.where((own ^ m) < (own ^ k), counts[m], 0)
+        for second in range(2):
+            at = ((label - begin) & (groups - 1)) + groups * second
+
+            @pl.when(at < counts[k])
+            def _():
+                arrival_ref[(begin + at) // groups] = 2 * (own ^ k) + second
+
+
+def arrivals(order, near, far):
+    scalar = pl.BlockSpec(memory_space=pltpu.SMEM)
+    return pl.pallas_call(
+        arrival_kernel,
+        in_specs=[scalar] * 5,
+        out_specs=scalar,
+        out_shape=jax.ShapeDtypeStruct((near.shape[1] // 2,), jnp.int32),
+    )(order, near, *far)
+
+
+def banded(raw_ref, big_ref):
+    chans = raw_ref.shape[0]
+    turned = raw_ref[...].astype(jnp.float32).T
+    blank = jnp.zeros((chans, chans), jnp.float32)
+    for t in range(big_ref.shape[0]):
+        strip = turned[3 * chans * t:3 * chans * (t + 1)]
+        parts = [
+            jnp.concatenate([strip[chans:], blank, blank], axis=0),
+            jnp.concatenate([strip, blank], axis=0),
+            jnp.concatenate([blank, strip], axis=0),
+            jnp.concatenate([blank, blank, strip[:2 * chans]], axis=0),
+        ]
+        for h in range(2):
+            both = jnp.concatenate(parts[2 * h:2 * h + 2], axis=1)
+            big_ref[t, :, 128 * h:128 * h + 128] = both.astype(jnp.bfloat16)
+
+
 def features_kernel(
     order_ref, near_ref, far1_ref, far2_ref, far3_ref, first_ref, vol0_ref, vol1_ref, vol2_ref, vol3_ref, below_ref, above_ref,
-    left_ref, right_ref, w1_ref, b1_ref, w2_ref, b2_ref,
-    sent_ref, arrival_ref, flip, taps, hidden, masks, pooled, staged, slots, sems,
+    left_ref, right_ref, raw1_ref, b1_ref, raw2_ref, b2_ref,
+    sent_ref, w1_ref, w2_ref, flip, taps, hidden, masks, pooled, staged, slots, sems,
 ):
     group = pl.program_id(0)
     last = group == pl.num_programs(0) - 1
@@ -62,40 +120,19 @@
 
     own = lax.axis_index("xy")
     groups = 4 * near_ref.shape[0]
-    fars = (near_ref, far1_ref, far2_ref, far3_ref)
 
     def route():
-        counts = []
-        for k in range(groups):
-            marks = fars[k // 4]
-            count = marks[k % 4, 0]
-            for j in range(1, columns):
-                count = count + marks[k % 4, j]
-            counts.append(count)
+        counts = counted((near_ref, far1_ref, far2_ref, far3_ref))
         start = jnp.int32(0)
         for k in range(1, groups):
             start = start + jnp.where((own ^ k) < own, counts[k], 0)
-        rank = jnp.int32(0)
         for j in range(columns):
             full = near_ref[0, j]
-            to = order_ref[0, (start + rank) & (groups - 1)]
-            slots[j] = jnp.where(full > 0, 2 * to + (rank >= groups).astype(jnp.int32), -1)
-            rank = rank + full
-        label = jnp.int32(0)
-        for i in range(groups):
-            label = label + jnp.where(order_ref[0, i] == own, i, 0)
-        for k in range(groups):
-            begin = jnp.int32(0)
-            for m in range(groups):
-                if m != k:
-                    begin = begin + jnp.where((own ^ m) < (own ^ k), counts[m], 0)
-            ahead = (label - begin) & (groups - 1)
-            for second in range(2):
-                at = ahead + groups * second
-
-                @pl.when(at < counts[k])
-                def _():
-                    arrival_ref[(begin + at) // groups] = 2 * (own ^ k) + second
+            to = order_ref[0, start & (groups - 1)]
+            begin = start if j == 0 else begin
+            second = (start - begin >= groups).astype(jnp.int32)
+            slots[j] = jnp.where(full > 0, 2 * to + second, -1)
+            start = start + full
 
     def turn_pieces(source, at_rim):
         def piece(j):
@@ -229,6 +266,8 @@
             own > 0, own < groups - 1,
         ]
         route()
+        banded(raw1_ref, w1_ref)
+        banded(raw2_ref, w2_ref)
 
         def inside(i):
             keep = None
@@ -341,12 +380,11 @@
             whole(below), whole(above), whole(left), whole(right),
             whole(w1), whole(b1), whole(w2), whole(b2),
         ],
-        out_specs=[pl.BlockSpec(memory_space=pl.ANY), scalar],
-        out_shape=[
-            jax.ShapeDtypeStruct((2 * groups, chans, 512), jnp.bfloat16),
-            jax.ShapeDtypeStruct((columns // 2,), jnp.int32),
-        ],
+        out_specs=pl.BlockSpec(memory_space=pl.ANY),
+        out_shape=jax.ShapeDtypeStruct((2 * groups, chans, 512), jnp.bfloat16),
         scratch_shapes=[
+            pltpu.VMEM((3, 256, 256), jnp.bfloat16),
+            pltpu.VMEM((9, 256, 256), jnp.bfloat16),
             pltpu.VMEM((FRONT + SEG * (4 * runs + PAD) + 8, 128), jnp.float32),
             pltpu.VMEM((2, 2, rows + 4 * SEG, 256), jnp.bfloat16),
             pltpu.VMEM((9, rows + 2 * SEG, 256), jnp.bfloat16),
@@ -364,19 +402,6 @@
       w1, b1, w2, b2)
 
 
-def banded(weight, taps):
-    chans = weight.shape[0]
-    parts = weight.reshape(chans, taps, 3, chans).transpose(1, 2, 3, 0)
-    blank = jnp.zeros_like(parts[:, 0])
-    rows = [
-        jnp.concatenate(
-            [parts[:, x - to + 1] if 0 <= x - to + 1 < 3 else blank for to in range(4)], axis=2
-        )
-        for x in range(4)
-    ]
-    return jnp.concatenate(rows, axis=1)
-
-
 def per_device(volume, occupancy, device_order, weight_one, bias_one, weight_two, bias_two):
     layers, chans, lanes = volume.shape
     columns = occupancy.shape[1]
@@ -406,11 +431,11 @@
     right = shift(edge(0, tissue_row[0]), "xy", -1)
     far = [swap(near, 4 * k) for k in (1, 2, 3)]
 
-    w1, w2 = banded(weight_one, 3), banded(weight_two, 9)
     b1, b2 = jnp.tile(bias_one, 4)[None], jnp.tile(bias_two, 4)[None]
-    sent, arrival = local_features(
-        device_order, near, far, volume, below, above, left, right, w1, b1, w2, b2
+    sent = local_features(
+        device_order, near, far, volume, below, above, left, right, weight_one, b1, weight_two, b2
     )
+    arrival = arrivals(device_order, near, far)
     arrived = lax.all_to_all(sent, "xy", split_axis=0, concat_axis=0, tiled=True)
     return jnp.take(arrived, arrival, axis=0, mode="clip")
 

time: 120 us -> 115 us (0.958)
  waiting for transfers between devices: 32.9 us -> 28.9 us
  other arithmetic: 6.78 us -> 4.58 us
    concatenate x2 -> x0, other arithmetic: 3.47 us -> none  [banded(): return jnp.concatenate(rows, axis=1)]
    all_to_all x1, waiting for transfers between devices: 29 us -> 26.2 us  [per_device(): lax.all_to_all(sent, 'xy', split_axis=0, concat_axis=0, tiled=True)]
    reshape x3 -> x0, local copies, waits for them, and re-layouts: 2.45 us -> none  [banded(): parts = weight.reshape(chans, taps, 3, chans).transpose(1, 2, 3, 0)]
    pallas_call x0 -> x1, Pallas kernels: none -> 2.06 us  [arrivals(): pl.pallas_call(arrival_kernel, in_specs=[scalar] * 5, out_specs=scalar, o...]
    unnamed x9 -> x14, local copies, waits for them, and re-layouts: 1.06 us -> 2.49 us
    another operation x4, local copies, waits for them, and re-layouts: 0.17 us -> 1.48 us  [per_device(): b1, b2 = (jnp.tile(bias_one, 4)[None], jnp.tile(bias_two, 4)[None])]
    ppermute x6, waiting for transfers between devices: 3.97 us -> 2.66 us  [swap(): return lax.ppermute(value, 'xy', [(i, i ^ k) for i in range(groups)])]
  transfers between devices with their start and end apart: 11 -> 11, of which waited for: 3 -> 2; matrix products, arithmetic and copies ran while one was open for 11% -> 8% of each run, Pallas kernels for 0% -> 2%
where the time goes in v2:
time: 115 us
  Pallas kernels  46.4 us (40%)
  waiting for transfers between devices  28.9 us (25%)
  starting transfers between devices  25.2 us (22%)
  local copies, waits for them, and re-layouts  8.1 us (7%)
  other arithmetic  4.58 us (4%)
  between operations  1.49 us (1%)
    pallas_call x1, Pallas kernels, local_features(): pl.pallas_call(features_kernel, grid=(pairs // 4,), in_specs=[scalar, sca...  44.4 us
    all_to_all x1, waiting for transfers between devices, per_device(): lax.all_to_all(sent, 'xy', split_axis=0, concat_axis=0, tiled=True)  26.2 us
    ppermute x6, starting transfers between devices, swap(): return lax.ppermute(value, 'xy', [(i, i ^ k) for i in range(groups)])  12.6 us
    ppermute x4, starting transfers between devices, shift(): return lax.ppermute(value, axis, pairs)  8.7 us
    all_to_all x1, starting transfers between devices, per_device(): lax.all_to_all(sent, 'xy', split_axis=0, concat_axis=0, tiled=True)  3.88 us
    ppermute x6, waiting for transfers between devices, swap(): return lax.ppermute(value, 'xy', [(i, i ^ k) for i in range(groups)])  2.66 us
    unnamed x14, local copies, waits for them, and re-layouts  2.49 us
  transfers between devices with their start and end apart: 11, of which 2 were waited for; matrix products, arithmetic and copies ran while one was open for 8% of the time, Pallas kernels for 2%

profile of v2, /device:TPU:0, one launch (start us, length us, event | category | flops | bytes accessed | tf_op | source)
XLA Modules:
  0.0 114.7 jit_solution(18103037061671978446)
XLA Ops:
  0.0 4.1 %collective-permute-start.2 = (s32[1,20]{1,0:T(1,128)}, s32[1,20]{1,0:T(1,128)S(1)}, u32[]{:S(2)}, u32[]{:S(2)}) collective-permute-start(s32[1,20]{1,0:T(1,128)} %param.8), channel_id=1, source_target_pairs={{0,3},{1,2},{2,1},{3,0},{4,7},{5,6},{6,5},{7,4},{8,11},{9,10},{10,... | collective-permute-start | bytes 248 | tf_op jit(solution)/shard_map/ppermute | solution.py:412
  4.1 0.9 collective-permute-start
  5.0 0.7 compare_bitcast_fusion
  5.8 1.1 slice_select_fusion.2
  6.9 1.3 %collective-permute-start.7 = (bf16[1,64,2560]{2,1,0:T(8,128)(2,1)S(1)}, bf16[1,64,2560]{2,1,0:T(8,128)(2,1)S(1)}, u32[]{:S(2)}, u32[]{:S(2)}) collective-permute-start(bf16[1,64,2560]{2,1,0:T(8,128)(2,1)S(1)} %get-tuple-element.5), channel_id=1, source_target_pairs={{16,0},{32,16},{48,32},{64,48},{80,64},{96,80},{112,96},{17,1},{33... | collective-permute-start | bytes 983048 | tf_op jit(solution)/shard_map/ppermute | solution.py:17
  8.2 3.1 %collective-permute-start.6 = (bf16[1,64,2560]{2,1,0:T(8,128)(2,1)S(1)}, bf16[1,64,2560]{2,1,0:T(8,128)(2,1)S(1)}, u32[]{:S(2)}, u32[]{:S(2)}) collective-permute-start(bf16[1,64,2560]{2,1,0:T(8,128)(2,1)S(1)} %get-tuple-element.6), channel_id=1, source_target_pairs={{0,16},{16,32},{32,48},{48,64},{64,80},{80,96},{96,112},{1,17},{17... | collective-permute-start | bytes 983048 | tf_op jit(solution)/shard_map/ppermute | solution.py:17
  11.2 1.3 %fusion.2 = (s32[1,1]{1,0:T(1,128)}, s32[1,1]{1,0:T(1,128)}) fusion(s32[1,20]{1,0:T(1,128)} %param.8), kind=kLoop, calls=%fused_computation.15 | loop fusion | bytes 16 | tf_op jit(solution)/shard_map/slice | solution.py:431
  13.9 1.4 %slice_select_fusion = (bf16[32,64,8]{2,1,0:T(8,128)(2,1)S(1)}, bf16[32,64,8]{2,1,0:T(8,128)(2,1)S(1)}) fusion(bf16[32,64,2560]{2,1,0:T(8,128)(2,1)} %vol3_ref.1, pred[]{:T(512)} %bitcast.9, pred[]{:T(512)} %bitcast.4), kind=kLoop, calls=%fused_computation.1 | loop fusion | flops 32768 | bytes 131074 | tf_op jit(solution)/shard_map/jit(_where)/select_n | solution.py:426
  15.3 0.2 copy.23
  15.5 0.1 reshape.54
  15.6 0.2 copy.19
  15.8 0.1 reshape.50
  16.2 0.1 fusion
  16.6 3.1 %collective-permute-start.8 = (bf16[17,8,128]{2,1,0:T(8,128)(2,1)S(1)}, bf16[17,8,128]{2,1,0:T(8,128)(2,1)S(1)}, u32[]{:S(2)}, u32[]{:S(2)}) collective-permute-start(bf16[17,8,128]{2,1,0:T(8,128)(2,1)S(1)} %pad_maximum_fusion), channel_id=1, source_target_pairs={{0,1},{1,2},{2,3},{3,4},{4,5},{5,6},{6,7},{7,8},{8,9},{9,10},{10,1... | collective-permute-start | bytes 104456 | tf_op jit(solution)/shard_map/ppermute | solution.py:17
  19.7 1.3 %collective-permute-start.9 = (bf16[17,8,128]{2,1,0:T(8,128)(2,1)S(1)}, bf16[17,8,128]{2,1,0:T(8,128)(2,1)S(1)}, u32[]{:S(2)}, u32[]{:S(2)}) collective-permute-start(bf16[17,8,128]{2,1,0:T(8,128)(2,1)S(1)} %pad_maximum_fusion.1), channel_id=1, source_target_pairs={{1,0},{2,1},{3,2},{4,3},{5,4},{6,5},{7,6},{8,7},{9,8},{10,9},{11,1... | collective-permute-start | bytes 104456 | tf_op jit(solution)/shard_map/ppermute | solution.py:17
  21.1 0.7 pad_add_fusion.near_ref
  21.7 6.7 %collective-permute-start.5 = (s32[4,20]{1,0:T(4,128)S(1)}, s32[4,20]{1,0:T(4,128)S(1)}, u32[]{:S(2)}, u32[]{:S(2)}) collective-permute-start(s32[4,20]{1,0:T(4,128)S(1)} %pad_add_fusion.near_ref), channel_id=1, source_target_pairs={{0,12},{1,13},{2,14},{3,15},{4,8},{5,9},{6,10},{7,11},{8,4},{9,5},... | collective-permute-start | bytes 968 | tf_op jit(solution)/shard_map/ppermute | solution.py:412
  28.4 0.6 collective-permute-start.4
  29.0 0.3 collective-permute-start.3
  29.4 0.7 tile.4
  30.1 0.7 tile.5
  30.8 0.1 broadcast_in_dim_tile.7.b2_ref
  30.8 2.7 %collective-permute-done.4.far2_ref = s32[4,20]{1,0:T(4,128)S(1)} collective-permute-done((s32[4,20]{1,0:T(4,128)S(1)}, s32[4,20]{1,0:T(4,128)S(1)}, u32[]{:S(2)}, u32[]{:S(2)}) %collective-permute-start.4) | collective-permute-done | bytes 352 | tf_op jit(solution)/shard_map/ppermute | solution.py:412
  33.5 0.6 copy-done.4
  34.2 0.9 copy-done.5
  35.1 0.9 copy-done.6
  36.0 44.4 %shard_map.73 = bf16[32,64,512]{2,1,0:T(8,128)(2,1)} custom-call(s32[1,16]{1,0:T(1,128)S(1)} %copy-done.4, s32[4,20]{1,0:T(4,128)S(1)} %pad_add_fusion.near_ref, s32[4,20]{1,0:T(4,128)S(1)} %collective-permute-done.3.far1_ref, s32[4,20]{1,0:T(4,128)S(1)} %collective-permute-done.4.far2_ref, s32[4,20]{1,0:T(4,128)S(1)} %collective-permute-done.5.far3_ref, ...), custom_call_target="tpu_custom_call" | custom-call | flops 32999999488 | bytes 16000000 | tf_op jit(solution)/shard_map/pallas_call | solution.py:373
  80.4 3.9 %all-to-all-start = ((bf16[32,64,512]{2,1,0:T(8,128)(2,1)}), bf16[32,64,512]{2,1,0:T(8,128)(2,1)S(1)}, u32[]{:S(2)}, u32[]{:S(2)}) async-start(bf16[32,64,512]{2,1,0:T(8,128)(2,1)} %shard_map.73), calls=%async_computation | async-start | bytes 4194304 | tf_op jit(solution)/shard_map/all_to_all | solution.py:439
  84.3 2.1 %shard_map.74 = s32[10]{0:T(128)} custom-call(s32[1,16]{1,0:T(1,128)} %order_ref.3, s32[4,20]{1,0:T(4,128)} %copy-done, s32[4,20]{1,0:T(4,128)} %copy-done.3, s32[4,20]{1,0:T(4,128)} %copy-done.2, s32[4,20]{1,0:T(4,128)} %copy-done.1), custom_call_target="tpu_custom_call" | custom-call | tf_op jit(solution)/shard_map/pallas_call | solution.py:81
  86.4 0.6 pad_clamp_fusion
  87.0 26.2 %all-to-all-done = bf16[32,64,512]{2,1,0:T(8,128)(2,1)S(1)} async-done(((bf16[32,64,512]{2,1,0:T(8,128)(2,1)}), bf16[32,64,512]{2,1,0:T(8,128)(2,1)S(1)}, u32[]{:S(2)}, u32[]{:S(2)}) %all-to-all-start) | async-done | bytes 2097184 | tf_op jit(solution)/shard_map/all_to_all | solution.py:439
  113.2 1.5 %gather_fusion = bf16[10,64,512]{2,1,0:T(8,128)(2,1)} fusion(bf16[32,64,512]{2,1,0:T(8,128)(2,1)S(1)} %all-to-all-done, s32[1024]{0:T(1024)S(1)} %pad_clamp_fusion), kind=kCustom, calls=%fused_computation | custom fusion | bytes 1310760 | tf_op jit(solution)/shard_map/jit(_take)/gather | solution.py:440
  (36 shorter events, 0.8 us)
Async XLA Ops:
  0.0 21.0 %collective-permute-start.2 = (s32[1,20]{1,0:T(1,128)}, s32[1,20]{1,0:T(1,128)S(1)}, u32[]{:S(2)}, u32[]{:S(2)}) collective-permute-start(s32[1,20]{1,0:T(1,128)} %param.8), channel_id=1, source_target_pairs={{0,3},{1,2},{2,1},{3,0},{4,7},{5,6},{6,5},{7,4},{8,11},{9,10},{10,... | collective-permute-start | bytes 248 | tf_op jit(solution)/shard_map/ppermute | solution.py:412
  4.1 16.9 %collective-permute-start.1 = (s32[1,20]{1,0:T(1,128)}, s32[1,20]{1,0:T(1,128)S(1)}, u32[]{:S(2)}, u32[]{:S(2)}) collective-permute-start(s32[1,20]{1,0:T(1,128)} %param.8), channel_id=1, source_target_pairs={{0,2},{1,3},{2,0},{3,1},{4,6},{5,7},{6,4},{7,5},{8,10},{9,11},{10,... | collective-permute-start | bytes 248 | tf_op jit(solution)/shard_map/ppermute | solution.py:412
  4.1 16.9 %collective-permute-start = (s32[1,20]{1,0:T(1,128)}, s32[1,20]{1,0:T(1,128)S(1)}, u32[]{:S(2)}, u32[]{:S(2)}) collective-permute-start(s32[1,20]{1,0:T(1,128)} %param.8), channel_id=1, source_target_pairs={{0,1},{1,0},{2,3},{3,2},{4,5},{5,4},{6,7},{7,6},{8,9},{9,8},{10,11... | collective-permute-start | bytes 248 | tf_op jit(solution)/shard_map/ppermute | solution.py:412
  6.9 9.0 %collective-permute-start.7 = (bf16[1,64,2560]{2,1,0:T(8,128)(2,1)S(1)}, bf16[1,64,2560]{2,1,0:T(8,128)(2,1)S(1)}, u32[]{:S(2)}, u32[]{:S(2)}) collective-permute-start(bf16[1,64,2560]{2,1,0:T(8,128)(2,1)S(1)} %get-tuple-element.5), channel_id=1, source_target_pairs={{16,0},{32,16},{48,32},{64,48},{80,64},{96,80},{112,96},{17,1},{33... | collective-permute-start | bytes 983048 | tf_op jit(solution)/shard_map/ppermute | solution.py:17
  8.2 8.0 %collective-permute-start.6 = (bf16[1,64,2560]{2,1,0:T(8,128)(2,1)S(1)}, bf16[1,64,2560]{2,1,0:T(8,128)(2,1)S(1)}, u32[]{:S(2)}, u32[]{:S(2)}) collective-permute-start(bf16[1,64,2560]{2,1,0:T(8,128)(2,1)S(1)} %get-tuple-element.6), channel_id=1, source_target_pairs={{0,16},{16,32},{32,48},{48,64},{64,80},{80,96},{96,112},{1,17},{17... | collective-permute-start | bytes 983048 | tf_op jit(solution)/shard_map/ppermute | solution.py:17
  16.6 16.9 %collective-permute-start.8 = (bf16[17,8,128]{2,1,0:T(8,128)(2,1)S(1)}, bf16[17,8,128]{2,1,0:T(8,128)(2,1)S(1)}, u32[]{:S(2)}, u32[]{:S(2)}) collective-permute-start(bf16[17,8,128]{2,1,0:T(8,128)(2,1)S(1)} %pad_maximum_fusion), channel_id=1, source_target_pairs={{0,1},{1,2},{2,3},{3,4},{4,5},{5,6},{6,7},{7,8},{8,9},{9,10},{10,1... | collective-permute-start | bytes 104456 | tf_op jit(solution)/shard_map/ppermute | solution.py:17
  19.7 13.8 %collective-permute-start.9 = (bf16[17,8,128]{2,1,0:T(8,128)(2,1)S(1)}, bf16[17,8,128]{2,1,0:T(8,128)(2,1)S(1)}, u32[]{:S(2)}, u32[]{:S(2)}) collective-permute-start(bf16[17,8,128]{2,1,0:T(8,128)(2,1)S(1)} %pad_maximum_fusion.1), channel_id=1, source_target_pairs={{1,0},{2,1},{3,2},{4,3},{5,4},{6,5},{7,6},{8,7},{9,8},{10,9},{11,1... | collective-permute-start | bytes 104456 | tf_op jit(solution)/shard_map/ppermute | solution.py:17
  21.7 58.7 %copy-start = (s32[4,20]{1,0:T(4,128)}, s32[4,20]{1,0:T(4,128)S(1)}, u32[]{:S(2)}) copy-start(s32[4,20]{1,0:T(4,128)S(1)} %pad_add_fusion.near_ref) | copy-start | bytes 964
  21.7 9.1 %collective-permute-start.5 = (s32[4,20]{1,0:T(4,128)S(1)}, s32[4,20]{1,0:T(4,128)S(1)}, u32[]{:S(2)}, u32[]{:S(2)}) collective-permute-start(s32[4,20]{1,0:T(4,128)S(1)} %pad_add_fusion.near_ref), channel_id=1, source_target_pairs={{0,12},{1,13},{2,14},{3,15},{4,8},{5,9},{6,10},{7,11},{8,4},{9,5},... | collective-permute-start | bytes 968 | tf_op jit(solution)/shard_map/ppermute | solution.py:412
  28.4 5.1 %collective-permute-start.4 = (s32[4,20]{1,0:T(4,128)S(1)}, s32[4,20]{1,0:T(4,128)S(1)}, u32[]{:S(2)}, u32[]{:S(2)}) collective-permute-start(s32[4,20]{1,0:T(4,128)S(1)} %pad_add_fusion.near_ref), channel_id=1, source_target_pairs={{0,8},{1,9},{2,10},{3,11},{4,12},{5,13},{6,14},{7,15},{8,0},{9,1},... | collective-permute-start | bytes 968 | tf_op jit(solution)/shard_map/ppermute | solution.py:412
  29.0 4.5 %collective-permute-start.3 = (s32[4,20]{1,0:T(4,128)S(1)}, s32[4,20]{1,0:T(4,128)S(1)}, u32[]{:S(2)}, u32[]{:S(2)}) collective-permute-start(s32[4,20]{1,0:T(4,128)S(1)} %pad_add_fusion.near_ref), channel_id=1, source_target_pairs={{0,4},{1,5},{2,6},{3,7},{4,0},{5,1},{6,2},{7,3},{8,12},{9,13},{10,... | collective-permute-start | bytes 968 | tf_op jit(solution)/shard_map/ppermute | solution.py:412
  30.8 49.6 %copy-start.1 = (s32[4,20]{1,0:T(4,128)}, s32[4,20]{1,0:T(4,128)S(1)}, u32[]{:S(2)}) copy-start(s32[4,20]{1,0:T(4,128)S(1)} %collective-permute-done.5.far3_ref) | copy-start | bytes 964
  33.5 46.9 %copy-start.2 = (s32[4,20]{1,0:T(4,128)}, s32[4,20]{1,0:T(4,128)S(1)}, u32[]{:S(2)}) copy-start(s32[4,20]{1,0:T(4,128)S(1)} %collective-permute-done.4.far2_ref) | copy-start | bytes 964
  33.5 46.9 %copy-start.3 = (s32[4,20]{1,0:T(4,128)}, s32[4,20]{1,0:T(4,128)S(1)}, u32[]{:S(2)}) copy-start(s32[4,20]{1,0:T(4,128)S(1)} %collective-permute-done.3.far1_ref) | copy-start | bytes 964
  33.5 0.7 copy-start.4
  34.2 0.9 copy-start.5
  35.1 0.9 copy-start.6
  80.4 32.8 %all-to-all-start = ((bf16[32,64,512]{2,1,0:T(8,128)(2,1)}), bf16[32,64,512]{2,1,0:T(8,128)(2,1)S(1)}, u32[]{:S(2)}, u32[]{:S(2)}) async-start(bf16[32,64,512]{2,1,0:T(8,128)(2,1)} %shard_map.73), calls=%async_computation | async-start | bytes 4194304 | tf_op jit(solution)/shard_map/all_to_all | solution.py:439

commit v3 on v2

--- a/solution.py
+++ b/solution.py
@@ -105,8 +105,8 @@
 
 def features_kernel(
     order_ref, near_ref, far1_ref, far2_ref, far3_ref, first_ref, vol0_ref, vol1_ref, vol2_ref, vol3_ref, below_ref, above_ref,
-    left_ref, right_ref, raw1_ref, b1_ref, raw2_ref, b2_ref,
-    sent_ref, w1_ref, w2_ref, flip, taps, hidden, masks, pooled, staged, slots, sems,
+    left_ref, right_ref, raw1_ref, bias1_ref, raw2_ref, bias2_ref,
+    sent_ref, b1_ref, b2_ref, w1_ref, w2_ref, flip, taps, hidden, masks, pooled, staged, slots, sems,
 ):
     group = pl.program_id(0)
     last = group == pl.num_programs(0) - 1
@@ -266,6 +266,8 @@
             own > 0, own < groups - 1,
         ]
         route()
+        for bias_ref, b_ref in ((bias1_ref, b1_ref), (bias2_ref, b2_ref)):
+            b_ref[...] = jnp.concatenate([bias_ref[...]] * 4, axis=1)
         banded(raw1_ref, w1_ref)
         banded(raw2_ref, w2_ref)
 
@@ -383,6 +385,8 @@
         out_specs=pl.BlockSpec(memory_space=pl.ANY),
         out_shape=jax.ShapeDtypeStruct((2 * groups, chans, 512), jnp.bfloat16),
         scratch_shapes=[
+            pltpu.VMEM((1, 4 * chans), jnp.float32),
+            pltpu.VMEM((1, 4 * chans), jnp.float32),
             pltpu.VMEM((3, 256, 256), jnp.bfloat16),
             pltpu.VMEM((9, 256, 256), jnp.bfloat16),
             pltpu.VMEM((FRONT + SEG * (4 * runs + PAD) + 8, 128), jnp.float32),
@@ -394,7 +398,7 @@
             pltpu.SMEM((columns,), jnp.int32),
             pltpu.SemaphoreType.DMA((columns,)),
         ],
-        compiler_params=pltpu.CompilerParams(vmem_limit_bytes=48 << 20),
+        compiler_params=pltpu.CompilerParams(vmem_limit_bytes=62 << 20),
         cost_estimate=pl.CostEstimate(
             flops=33_000_000_000, bytes_accessed=16_000_000, transcendentals=0
         ),
@@ -431,7 +435,7 @@
     right = shift(edge(0, tissue_row[0]), "xy", -1)
     far = [swap(near, 4 * k) for k in (1, 2, 3)]
 
-    b1, b2 = jnp.tile(bias_one, 4)[None], jnp.tile(bias_two, 4)[None]
+    b1, b2 = bias_one[None], bias_two[None]
     sent = local_features(
         device_order, near, far, volume, below, above, left, right, weight_one, b1, weight_two, b2
     )

time: 115 us -> 115 us (level)
  local copies, waits for them, and re-layouts: 8.1 us -> 4.79 us
  waiting for transfers between devices: 28.9 us -> 30.4 us
    unnamed x14 -> x16, local copies, waits for them, and re-layouts: 2.49 us -> 0.59 us
    ppermute x6, waiting for transfers between devices: 2.66 us -> 4.15 us  [swap(): return lax.ppermute(value, 'xy', [(i, i ^ k) for i in range(groups)])]
    another operation x4 -> x0, local copies, waits for them, and re-layouts: 1.48 us -> none  [per_device(): b1, b2 = (jnp.tile(bias_one, 4)[None], jnp.tile(bias_two, 4)[None])]
  transfers between devices with their start and end apart: 11 -> 11, of which waited for: 2 -> 3; matrix products, arithmetic and copies ran while one was open for 8% -> 6% of each run, Pallas kernels for 2% -> 2%
where the time goes in v3:
time: 115 us; the launch traced here: 114 us
  Pallas kernels  47.4 us (41%)
  waiting for transfers between devices  30.4 us (26%)
  starting transfers between devices  25.4 us (22%)
  local copies, waits for them, and re-layouts  4.79 us (4%)
  other arithmetic  4.62 us (4%)
  between operations  1.57 us (1%)
    pallas_call x1, Pallas kernels, local_features(): pl.pallas_call(features_kernel, grid=(pairs // 4,), in_specs=[scalar, sca...  45.3 us
    all_to_all x1, waiting for transfers between devices, per_device(): lax.all_to_all(sent, 'xy', split_axis=0, concat_axis=0, tiled=True)  26.2 us
    ppermute x6, starting transfers between devices, swap(): return lax.ppermute(value, 'xy', [(i, i ^ k) for i in range(groups)])  12.6 us
    ppermute x4, starting transfers between devices, shift(): return lax.ppermute(value, axis, pairs)  8.7 us
    ppermute x6, waiting for transfers between devices, swap(): return lax.ppermute(value, 'xy', [(i, i ^ k) for i in range(groups)])  4.15 us
    all_to_all x1, starting transfers between devices, per_device(): lax.all_to_all(sent, 'xy', split_axis=0, concat_axis=0, tiled=True)  4.08 us
  transfers between devices with their start and end apart: 11, of which 3 were waited for; matrix products, arithmetic and copies ran while one was open for 6% of the time, Pallas kernels for 2%

profile of v3, /device:TPU:0, one launch (start us, length us, event | category | flops | bytes accessed | tf_op | source)
XLA Modules:
  0.0 114.1 jit_solution(12692609197581976353)
XLA Ops:
  0.0 4.1 %collective-permute-start.2 = (s32[1,20]{1,0:T(1,128)}, s32[1,20]{1,0:T(1,128)S(1)}, u32[]{:S(2)}, u32[]{:S(2)}) collective-permute-start(s32[1,20]{1,0:T(1,128)} %param.8), channel_id=1, source_target_pairs={{0,3},{1,2},{2,1},{3,0},{4,7},{5,6},{6,5},{7,4},{8,11},{9,10},{10,... | collective-permute-start | bytes 248 | tf_op jit(solution)/shard_map/ppermute | solution.py:416
  4.1 0.9 collective-permute-start
  5.0 0.7 compare_bitcast_fusion
  5.7 0.1 broadcast_bitcast_fusion
  5.8 1.1 slice_select_fusion.2
  6.9 1.3 %collective-permute-start.7 = (bf16[1,64,2560]{2,1,0:T(8,128)(2,1)S(1)}, bf16[1,64,2560]{2,1,0:T(8,128)(2,1)S(1)}, u32[]{:S(2)}, u32[]{:S(2)}) collective-permute-start(bf16[1,64,2560]{2,1,0:T(8,128)(2,1)S(1)} %get-tuple-element.5), channel_id=1, source_target_pairs={{16,0},{32,16},{48,32},{64,48},{80,64},{96,80},{112,96},{17,1},{33... | collective-permute-start | bytes 983048 | tf_op jit(solution)/shard_map/ppermute | solution.py:17
  8.2 3.1 %collective-permute-start.6 = (bf16[1,64,2560]{2,1,0:T(8,128)(2,1)S(1)}, bf16[1,64,2560]{2,1,0:T(8,128)(2,1)S(1)}, u32[]{:S(2)}, u32[]{:S(2)}) collective-permute-start(bf16[1,64,2560]{2,1,0:T(8,128)(2,1)S(1)} %get-tuple-element.6), channel_id=1, source_target_pairs={{0,16},{16,32},{32,48},{48,64},{64,80},{80,96},{96,112},{1,17},{17... | collective-permute-start | bytes 983048 | tf_op jit(solution)/shard_map/ppermute | solution.py:17
  11.2 1.4 %fusion.2 = (s32[1,1]{1,0:T(1,128)}, s32[1,1]{1,0:T(1,128)}) fusion(s32[1,20]{1,0:T(1,128)} %param.8), kind=kLoop, calls=%fused_computation.15 | loop fusion | bytes 16 | tf_op jit(solution)/shard_map/slice | solution.py:435
  14.0 1.4 %slice_select_fusion = (bf16[32,64,8]{2,1,0:T(8,128)(2,1)S(1)}, bf16[32,64,8]{2,1,0:T(8,128)(2,1)S(1)}) fusion(bf16[32,64,2560]{2,1,0:T(8,128)(2,1)} %vol3_ref.1, pred[]{:T(512)} %bitcast.9, pred[]{:T(512)} %bitcast.4), kind=kLoop, calls=%fused_computation.1 | loop fusion | flops 32768 | bytes 131074 | tf_op jit(solution)/shard_map/jit(_where)/select_n | solution.py:430
  15.4 0.2 copy.23
  15.6 0.1 reshape.52
  15.7 0.2 copy.19
  15.9 0.1 reshape.48
  16.1 0.1 fusion.1
  16.3 0.1 fusion
  16.5 0.1 reshape.50
  16.7 0.1 reshape.46
  16.8 3.1 %collective-permute-start.8 = (bf16[17,8,128]{2,1,0:T(8,128)(2,1)S(1)}, bf16[17,8,128]{2,1,0:T(8,128)(2,1)S(1)}, u32[]{:S(2)}, u32[]{:S(2)}) collective-permute-start(bf16[17,8,128]{2,1,0:T(8,128)(2,1)S(1)} %pad_maximum_fusion), channel_id=1, source_target_pairs={{0,1},{1,2},{2,3},{3,4},{4,5},{5,6},{6,7},{7,8},{8,9},{9,10},{10,1... | collective-permute-start | bytes 104456 | tf_op jit(solution)/shard_map/ppermute | solution.py:17
  19.9 1.3 %collective-permute-start.9 = (bf16[17,8,128]{2,1,0:T(8,128)(2,1)S(1)}, bf16[17,8,128]{2,1,0:T(8,128)(2,1)S(1)}, u32[]{:S(2)}, u32[]{:S(2)}) collective-permute-start(bf16[17,8,128]{2,1,0:T(8,128)(2,1)S(1)} %pad_maximum_fusion.1), channel_id=1, source_target_pairs={{1,0},{2,1},{3,2},{4,3},{5,4},{6,5},{7,6},{8,7},{9,8},{10,9},{11,1... | collective-permute-start | bytes 104456 | tf_op jit(solution)/shard_map/ppermute | solution.py:17
  21.2 0.7 pad_add_fusion.near_ref
  21.9 6.7 %collective-permute-start.5 = (s32[4,20]{1,0:T(4,128)S(1)}, s32[4,20]{1,0:T(4,128)S(1)}, u32[]{:S(2)}, u32[]{:S(2)}) collective-permute-start(s32[4,20]{1,0:T(4,128)S(1)} %pad_add_fusion.near_ref), channel_id=1, source_target_pairs={{0,12},{1,13},{2,14},{3,15},{4,8},{5,9},{6,10},{7,11},{8,4},{9,5},... | collective-permute-start | bytes 968 | tf_op jit(solution)/shard_map/ppermute | solution.py:416
  28.6 0.6 collective-permute-start.4
  29.2 0.3 collective-permute-start.3
  29.5 0.6 collective-permute-done.5.far3_ref
  30.1 3.5 %collective-permute-done.4.far2_ref = s32[4,20]{1,0:T(4,128)S(1)} collective-permute-done((s32[4,20]{1,0:T(4,128)S(1)}, s32[4,20]{1,0:T(4,128)S(1)}, u32[]{:S(2)}, u32[]{:S(2)}) %collective-permute-start.4) | collective-permute-done | bytes 352 | tf_op jit(solution)/shard_map/ppermute | solution.py:416
  33.7 0.5 copy-done.4
  34.3 45.3 %shard_map.73 = bf16[32,64,512]{2,1,0:T(8,128)(2,1)} custom-call(s32[1,16]{1,0:T(1,128)} %order_ref.3, s32[4,20]{1,0:T(4,128)} %copy-done, s32[4,20]{1,0:T(4,128)} %copy-done.5, s32[4,20]{1,0:T(4,128)} %copy-done.4, s32[4,20]{1,0:T(4,128)} %copy-done.3, bf16[32,64,2560]{2,1,0:T(8,128)(2,1)} %vol3_ref.1, bf16[32,64,2560]{2,1,0:T(8,128)(2,1)} %vol3_ref.1, ...), custom_call_target="tpu_custom_call" | custom-call | flops 32999999488 | bytes 16000000 | tf_op jit(solution)/shard_map/pallas_call | solution.py:375
  79.6 4.1 %all-to-all-start = ((bf16[32,64,512]{2,1,0:T(8,128)(2,1)}), bf16[32,64,512]{2,1,0:T(8,128)(2,1)S(1)}, u32[]{:S(2)}, u32[]{:S(2)}) async-start(bf16[32,64,512]{2,1,0:T(8,128)(2,1)} %shard_map.73), calls=%async_computation | async-start | bytes 4194304 | tf_op jit(solution)/shard_map/all_to_all | solution.py:443
  83.7 2.1 %shard_map.74 = s32[10]{0:T(128)} custom-call(s32[1,16]{1,0:T(1,128)} %order_ref.3, s32[4,20]{1,0:T(4,128)} %copy-done, s32[4,20]{1,0:T(4,128)} %copy-done.5, s32[4,20]{1,0:T(4,128)} %copy-done.4, s32[4,20]{1,0:T(4,128)} %copy-done.3), custom_call_target="tpu_custom_call" | custom-call | tf_op jit(solution)/shard_map/pallas_call | solution.py:81
  85.8 0.7 pad_clamp_fusion
  86.4 26.2 %all-to-all-done = bf16[32,64,512]{2,1,0:T(8,128)(2,1)S(1)} async-done(((bf16[32,64,512]{2,1,0:T(8,128)(2,1)}), bf16[32,64,512]{2,1,0:T(8,128)(2,1)S(1)}, u32[]{:S(2)}, u32[]{:S(2)}) %all-to-all-start) | async-done | bytes 2097184 | tf_op jit(solution)/shard_map/all_to_all | solution.py:443
  112.7 1.5 %gather_fusion = bf16[10,64,512]{2,1,0:T(8,128)(2,1)} fusion(bf16[32,64,512]{2,1,0:T(8,128)(2,1)S(1)} %all-to-all-done, s32[1024]{0:T(1024)S(1)} %pad_clamp_fusion), kind=kCustom, calls=%fused_computation | custom fusion | bytes 1310760 | tf_op jit(solution)/shard_map/jit(_take)/gather | solution.py:444
  (34 shorter events, 0.5 us)
Async XLA Ops:
  0.0 21.2 %collective-permute-start.2 = (s32[1,20]{1,0:T(1,128)}, s32[1,20]{1,0:T(1,128)S(1)}, u32[]{:S(2)}, u32[]{:S(2)}) collective-permute-start(s32[1,20]{1,0:T(1,128)} %param.8), channel_id=1, source_target_pairs={{0,3},{1,2},{2,1},{3,0},{4,7},{5,6},{6,5},{7,4},{8,11},{9,10},{10,... | collective-permute-start | bytes 248 | tf_op jit(solution)/shard_map/ppermute | solution.py:416
  4.1 17.1 %collective-permute-start.1 = (s32[1,20]{1,0:T(1,128)}, s32[1,20]{1,0:T(1,128)S(1)}, u32[]{:S(2)}, u32[]{:S(2)}) collective-permute-start(s32[1,20]{1,0:T(1,128)} %param.8), channel_id=1, source_target_pairs={{0,2},{1,3},{2,0},{3,1},{4,6},{5,7},{6,4},{7,5},{8,10},{9,11},{10,... | collective-permute-start | bytes 248 | tf_op jit(solution)/shard_map/ppermute | solution.py:416
  4.1 17.1 %collective-permute-start = (s32[1,20]{1,0:T(1,128)}, s32[1,20]{1,0:T(1,128)S(1)}, u32[]{:S(2)}, u32[]{:S(2)}) collective-permute-start(s32[1,20]{1,0:T(1,128)} %param.8), channel_id=1, source_target_pairs={{0,1},{1,0},{2,3},{3,2},{4,5},{5,4},{6,7},{7,6},{8,9},{9,8},{10,11... | collective-permute-start | bytes 248 | tf_op jit(solution)/shard_map/ppermute | solution.py:416
  6.9 9.2 %collective-permute-start.7 = (bf16[1,64,2560]{2,1,0:T(8,128)(2,1)S(1)}, bf16[1,64,2560]{2,1,0:T(8,128)(2,1)S(1)}, u32[]{:S(2)}, u32[]{:S(2)}) collective-permute-start(bf16[1,64,2560]{2,1,0:T(8,128)(2,1)S(1)} %get-tuple-element.5), channel_id=1, source_target_pairs={{16,0},{32,16},{48,32},{64,48},{80,64},{96,80},{112,96},{17,1},{33... | collective-permute-start | bytes 983048 | tf_op jit(solution)/shard_map/ppermute | solution.py:17
  8.2 8.1 %collective-permute-start.6 = (bf16[1,64,2560]{2,1,0:T(8,128)(2,1)S(1)}, bf16[1,64,2560]{2,1,0:T(8,128)(2,1)S(1)}, u32[]{:S(2)}, u32[]{:S(2)}) collective-permute-start(bf16[1,64,2560]{2,1,0:T(8,128)(2,1)S(1)} %get-tuple-element.6), channel_id=1, source_target_pairs={{0,16},{16,32},{32,48},{48,64},{64,80},{80,96},{96,112},{1,17},{17... | collective-permute-start | bytes 983048 | tf_op jit(solution)/shard_map/ppermute | solution.py:17
  16.1 17.6 %copy-start.1 = (bf16[1,64,2560]{2,1,0:T(8,128)(2,1)}, bf16[1,64,2560]{2,1,0:T(8,128)(2,1)S(1)}, u32[]{:S(2)}) copy-start(bf16[1,64,2560]{2,1,0:T(8,128)(2,1)S(1)} %collective-permute-done.7.above_ref) | copy-start | bytes 983044
  16.3 17.4 %copy-start.2 = (bf16[1,64,2560]{2,1,0:T(8,128)(2,1)}, bf16[1,64,2560]{2,1,0:T(8,128)(2,1)S(1)}, u32[]{:S(2)}) copy-start(bf16[1,64,2560]{2,1,0:T(8,128)(2,1)S(1)} %collective-permute-done.6.below_ref) | copy-start | bytes 983044
  16.8 16.9 %collective-permute-start.8 = (bf16[17,8,128]{2,1,0:T(8,128)(2,1)S(1)}, bf16[17,8,128]{2,1,0:T(8,128)(2,1)S(1)}, u32[]{:S(2)}, u32[]{:S(2)}) collective-permute-start(bf16[17,8,128]{2,1,0:T(8,128)(2,1)S(1)} %pad_maximum_fusion), channel_id=1, source_target_pairs={{0,1},{1,2},{2,3},{3,4},{4,5},{5,6},{6,7},{7,8},{8,9},{9,10},{10,1... | collective-permute-start | bytes 104456 | tf_op jit(solution)/shard_map/ppermute | solution.py:17
  19.9 13.8 %collective-permute-start.9 = (bf16[17,8,128]{2,1,0:T(8,128)(2,1)S(1)}, bf16[17,8,128]{2,1,0:T(8,128)(2,1)S(1)}, u32[]{:S(2)}, u32[]{:S(2)}) collective-permute-start(bf16[17,8,128]{2,1,0:T(8,128)(2,1)S(1)} %pad_maximum_fusion.1), channel_id=1, source_target_pairs={{1,0},{2,1},{3,2},{4,3},{5,4},{6,5},{7,6},{8,7},{9,8},{10,9},{11,1... | collective-permute-start | bytes 104456 | tf_op jit(solution)/shard_map/ppermute | solution.py:17
  21.9 11.8 %copy-start = (s32[4,20]{1,0:T(4,128)}, s32[4,20]{1,0:T(4,128)S(1)}, u32[]{:S(2)}) copy-start(s32[4,20]{1,0:T(4,128)S(1)} %pad_add_fusion.near_ref) | copy-start | bytes 964
  21.9 8.2 %collective-permute-start.5 = (s32[4,20]{1,0:T(4,128)S(1)}, s32[4,20]{1,0:T(4,128)S(1)}, u32[]{:S(2)}, u32[]{:S(2)}) collective-permute-start(s32[4,20]{1,0:T(4,128)S(1)} %pad_add_fusion.near_ref), channel_id=1, source_target_pairs={{0,12},{1,13},{2,14},{3,15},{4,8},{5,9},{6,10},{7,11},{8,4},{9,5},... | collective-permute-start | bytes 968 | tf_op jit(solution)/shard_map/ppermute | solution.py:416
  28.6 5.1 %collective-permute-start.4 = (s32[4,20]{1,0:T(4,128)S(1)}, s32[4,20]{1,0:T(4,128)S(1)}, u32[]{:S(2)}, u32[]{:S(2)}) collective-permute-start(s32[4,20]{1,0:T(4,128)S(1)} %pad_add_fusion.near_ref), channel_id=1, source_target_pairs={{0,8},{1,9},{2,10},{3,11},{4,12},{5,13},{6,14},{7,15},{8,0},{9,1},... | collective-permute-start | bytes 968 | tf_op jit(solution)/shard_map/ppermute | solution.py:416
  29.2 4.5 %collective-permute-start.3 = (s32[4,20]{1,0:T(4,128)S(1)}, s32[4,20]{1,0:T(4,128)S(1)}, u32[]{:S(2)}, u32[]{:S(2)}) collective-permute-start(s32[4,20]{1,0:T(4,128)S(1)} %pad_add_fusion.near_ref), channel_id=1, source_target_pairs={{0,4},{1,5},{2,6},{3,7},{4,0},{5,1},{6,2},{7,3},{8,12},{9,13},{10,... | collective-permute-start | bytes 968 | tf_op jit(solution)/shard_map/ppermute | solution.py:416
  30.1 3.6 %copy-start.3 = (s32[4,20]{1,0:T(4,128)}, s32[4,20]{1,0:T(4,128)S(1)}, u32[]{:S(2)}) copy-start(s32[4,20]{1,0:T(4,128)S(1)} %collective-permute-done.5.far3_ref) | copy-start | bytes 964
  33.6 0.6 copy-start.4
  33.7 0.6 copy-start.5
  33.7 0.6 copy-start.6
  33.7 0.6 copy-start.7
  79.6 33.0 %all-to-all-start = ((bf16[32,64,512]{2,1,0:T(8,128)(2,1)}), bf16[32,64,512]{2,1,0:T(8,128)(2,1)S(1)}, u32[]{:S(2)}, u32[]{:S(2)}) async-start(bf16[32,64,512]{2,1,0:T(8,128)(2,1)} %shard_map.73), calls=%async_computation | async-start | bytes 4194304 | tf_op jit(solution)/shard_map/all_to_all | solution.py:443
